TPU v7x, 256 devices: a whole 4x4x8 slice. The times are simulated.
256 devices in a mesh: wide: 8 (over x_lo, y), narrow: 32 (over z, x_hi, core).
Axes of the slice: x: 4 (x_hi: 2, x_lo: 2; x = x_hi * 2 + x_lo), y: 4, z: 8, core: 2. Of those that a mesh axis runs over, the one named last changes fastest.
Arguments:
- right_side: float32 [1024, 320, 128], P(('wide', 'narrow')), may hold values from -6 to 6
- fine_blocks: float32 [1024, 320, 320], P(('wide', 'narrow'))
- fine_inverses: float32 [1024, 320, 320], P(('wide', 'narrow')), as said below
- fine_lifts: float32 [6, 320, 80], replicated, may hold values from -0.625 to 0.625
- fine_coefs: float32 [1024, 6, 80], P(('wide', 'narrow')), may hold values from 0.1 to 0.4
- coarse_blocks: float32 [1024, 40, 40], P(('wide', 'narrow'))
- coarse_inverses: float32 [1024, 40, 40], P(('wide', 'narrow')), as said below
- coarse_lifts: float32 [6, 40, 20], replicated, may hold values from -1.25 to 1.25
- coarse_coefs: float32 [1024, 6, 20], P(('wide', 'narrow')), may hold values from 0.15 to 0.6
- neighbours: int32 [1024, 6], P(('wide', 'narrow')), may hold values from -1 to 1023, as said below
- counts: int32 [256], P(('wide', 'narrow')), may hold values from 2 to 4, as said below
Outputs:
- solution: float32 [1024, 320, 128], P(('wide', 'narrow'))
Inputs may be any that keep to these rules, and one draw needn't show every extreme that they name: Slots 0 to counts - 1 of a device are its live elements, the rest are empty. Some device has all 4 slots live and some has only 2. Each entry is -1 or the index of a live element; empty slots hold -1 on all faces. If neighbours[e, f] = g then neighbours[g, f xor 1] = e. Across faces 0 and 1 the neighbour lies on the same device or on the device one wide index lower (face 0) or higher (face 1) with the same narrow index; across faces 2 and 3 likewise along narrow; across faces 4 and 5 on the same device. For every pair of devices next to each other along either axis exactly 1 face crosses between them. `fine_inverses`: an approximate inverse of the element's fine block, as incomplete factors give it. `coarse_inverses`: an approximate inverse of the element's coarse block, as incomplete factors give it.
All inputs are finite; a program needn't handle non-finite values.
Results may differ from a plain program's by a relative error of at most 0.00022.
Values sent between devices are 32-bit elements; how exact they have to be, the bound alone decides.
A program may use at most 64 MiB of HBM per device.

v0:
```python
import jax
import jax.numpy as jnp
import numpy as np
from jax import lax
from jax.sharding import PartitionSpec as P

NVAR = 5
NODE1 = 4
PRE_SWEEPS = 2
POST_SWEEPS = 2
COARSE_SWEEPS = 4


damping = 0.8
highest = lax.Precision.HIGHEST


def with_halo(cells, sides, width):
    for axis, dim in sides:
        count = lax.axis_size(axis)
        ends = count - 1
        head = lax.slice_in_dim(cells, 0, width, axis=dim)
        tail = lax.slice_in_dim(cells, cells.shape[dim] - width, cells.shape[dim], axis=dim)
        cells = jnp.concatenate(
            [
                lax.ppermute(tail, axis, [(i, (i + 1) % count) for i in range(ends)]),
                cells,
                lax.ppermute(head, axis, [((i + 1) % count, i) for i in range(ends)]),
            ],
            axis=dim,
        )
    return cells


def prolong_table(node_count, variables):
    points = np.array([-1.0, -1.0 / np.sqrt(5.0), 1.0 / np.sqrt(5.0), 1.0])
    linear = np.stack([(1.0 - points) / 2.0, (1.0 + points) / 2.0], axis=1)
    tensor_hat = (
        linear[:, None, None, :, None, None]
        * linear[None, :, None, None, :, None]
        * linear[None, None, :, None, None, :]
    )
    tensor_hat = tensor_hat.reshape(node_count * node_count * node_count, 8)
    return np.kron(np.eye(variables), tensor_hat).astype(np.float32)


def block_apply(blocks, vectors):
    return jnp.einsum("epq,eqr->epr", blocks, vectors, precision=highest)


def lift_apply(face_lifts, face_coefs, nearby):
    return jnp.einsum(
        "fpq,efqr->epr", face_lifts, face_coefs[:, :, :, None] * nearby, precision=highest
    )


def face_traces(state_field, node_count):
    slot_count = state_field.shape[0]
    columns = state_field.shape[2]
    shaped = state_field.reshape(slot_count, NVAR, node_count, node_count, node_count, columns)
    last = node_count - 1
    layers = [
        shaped[:, :, 0],
        shaped[:, :, last],
        shaped[:, :, :, 0],
        shaped[:, :, :, last],
        shaped[:, :, :, :, 0],
        shaped[:, :, :, :, last],
    ]
    flat = [layer.reshape(slot_count, NVAR * node_count * node_count, columns) for layer in layers]
    return jnp.stack(flat, axis=1)


def pick_rows(candidates, row_index, weight):
    positions = jnp.arange(candidates.shape[0])
    selector = (row_index[:, None] == positions[None, :]).astype(jnp.float32) * weight[:, None]
    return jnp.einsum("ab,bqr->aqr", selector, candidates, precision=highest)


def gather_faces(traces, arrivals, present, pick_index):
    pieces = []
    for face_side in range(6):
        candidates = traces[:, face_side ^ 1]
        if arrivals[face_side] is not None:
            candidates = jnp.concatenate([candidates, arrivals[face_side]], axis=0)
        pieces.append(pick_rows(candidates, pick_index[:, face_side], present[:, face_side]))
    return jnp.stack(pieces, axis=1)


def decode(neighbours, device_id, slot_count):
    present = neighbours >= 0
    owner_device = jnp.where(present, neighbours // slot_count, -1)
    home_slot = jnp.where(present, neighbours % slot_count, 0)
    at_home = jnp.logical_and(present, owner_device == device_id)
    return (present, at_home, home_slot)


def fine_couple(state_field, face_lifts, face_coefs, node_count, present, at_home, home_slot):
    slot_count = state_field.shape[0]
    traces = face_traces(state_field, node_count)
    rim_wide = with_halo(jnp.stack([traces[:, 0], traces[:, 1]]), (("wide", 0),), 1)
    rim_narrow = with_halo(jnp.stack([traces[:, 2], traces[:, 3]]), (("narrow", 0),), 1)
    arrivals = [rim_wide[0], rim_wide[3], rim_narrow[0], rim_narrow[3], None, None]
    pick_index = jnp.where(at_home, home_slot, slot_count + home_slot)
    nearby = gather_faces(traces, arrivals, present.astype(jnp.float32), pick_index)
    return lift_apply(face_lifts, face_coefs, nearby)


def coarse_spread_couple(
    state_field, face_lifts, face_coefs, node_count, present, at_home, home_slot
):
    slot_count = state_field.shape[0]
    traces = face_traces(state_field, node_count)
    rim_wide = with_halo(jnp.stack([traces[:, 0], traces[:, 1]]), (("wide", 0),), 1)
    rim_narrow = with_halo(jnp.stack([traces[:, 2], traces[:, 3]]), (("narrow", 0),), 1)
    arrivals = [rim_wide[0], rim_wide[3], rim_narrow[0], rim_narrow[3], None, None]
    pick_index = jnp.where(at_home, home_slot, slot_count + home_slot)
    nearby = gather_faces(traces, arrivals, present.astype(jnp.float32), pick_index)
    return lift_apply(face_lifts, face_coefs, nearby)


def smooth(solution, rhs_live, blocks, inverses, couple_fn, sweeps):
    for sweep_index in range(sweeps):
        if solution is None:
            solution = damping * block_apply(inverses, rhs_live)
        else:
            residual = rhs_live - block_apply(blocks, solution) - couple_fn(solution)
            solution = solution + damping * block_apply(inverses, residual)
    return solution


def body(
    right_side,
    fine_blocks,
    fine_inverses,
    fine_lifts,
    fine_coefs,
    coarse_blocks,
    coarse_inverses,
    coarse_lifts,
    coarse_coefs,
    neighbours,
    counts,
):
    slot_count = right_side.shape[0]
    narrow_size = lax.axis_size("narrow")
    narrow_here = lax.axis_index("narrow")
    wide_here = lax.axis_index("wide")
    device_id = wide_here * narrow_size + narrow_here
    live_mask = (jnp.arange(slot_count) < counts[0]).astype(jnp.float32)
    rhs_live = right_side * live_mask[:, None, None]
    prolong = jnp.asarray(prolong_table(NODE1, NVAR))
    present, at_home, home_slot = decode(neighbours, device_id, slot_count)

    def fine_operator(state_field):
        return fine_couple(state_field, fine_lifts, fine_coefs, NODE1, present, at_home, home_slot)

    solution = smooth(None, rhs_live, fine_blocks, fine_inverses, fine_operator, PRE_SWEEPS)
    residual = rhs_live - block_apply(fine_blocks, solution) - fine_operator(solution)
    coarse_rhs = 0.25 * jnp.einsum("pq,epr->eqr", prolong, residual, precision=highest)

    def spread_operator(state_field):
        return coarse_spread_couple(
            state_field, coarse_lifts, coarse_coefs, 2, present, at_home, home_slot
        )

    coarse_solution = smooth(
        None, coarse_rhs, coarse_blocks, coarse_inverses, spread_operator, COARSE_SWEEPS
    )
    solution = solution + jnp.einsum("pq,eqr->epr", prolong, coarse_solution, precision=highest)
    solution = smooth(solution, rhs_live, fine_blocks, fine_inverses, fine_operator, POST_SWEEPS)
    return solution


def solution(mesh):
    placed = (
        P(("wide", "narrow"), None, None),
        P(("wide", "narrow"), None, None),
        P(("wide", "narrow"), None, None),
        P(),
        P(("wide", "narrow"), None, None),
        P(("wide", "narrow"), None, None),
        P(("wide", "narrow"), None, None),
        P(),
        P(("wide", "narrow"), None, None),
        P(("wide", "narrow"), None),
        P(("wide", "narrow")),
    )
    return jax.shard_map(
        body,
        mesh=mesh,
        in_specs=placed,
        out_specs=P(("wide", "narrow"), None, None),
        check_vma=False,
    )
```

profile of v0, /device:TPU:103, one launch (start us, length us, event | category | flops | bytes accessed | tf_op | source)
XLA Modules:
  0.0 191.5 jit_solution(17990389945694893769)
XLA Ops:
  0.8 3.7 %convolution_multiply_fusion.3 = f32[4,128,320]{1,2,0:T(8,128)S(1)} fusion(f32[4,320,320]{2,1,0:T(8,128)} %param.14, f32[4,320,128]{2,1,0:T(8,128)} %param.12, f32[4]{0:T(128)S(1)} %compare_convert_fusion), kind=kOutput, calls=%fused_computation.27 | convolution fusion | flops 629473280 | bytes 2949136 | tf_op jit(solution)/shard_map/epq,eqr->epr/dot_general | solution.py:48
  4.6 3.2 %collective-permute-start = (f32[1,4,80,128]{3,1,2,0:T(4,128)S(1)}, f32[1,4,80,128]{3,1,2,0:T(4,128)}, u32[]{:S(2)}, u32[]{:S(2)}) collective-permute-start(f32[1,4,80,128]{3,1,2,0:T(4,128)S(1)} %bitcast.545), channel_id=1, source_target_pairs={{0,32},{32,64},{64,96},{96,128},{128,160},{160,192},{192,224},{1,3... | collective-permute-start | bytes 491528 | tf_op jit(solution)/shard_map/ppermute | solution.py:26
  8.6 4.2 %collective-permute-start.1 = (f32[1,4,80,128]{3,1,2,0:T(4,128)}, f32[1,4,80,128]{3,1,2,0:T(4,128)}, u32[]{:S(2)}, u32[]{:S(2)}) collective-permute-start(f32[1,4,80,128]{3,1,2,0:T(4,128)} %bitcast.12), channel_id=1, source_target_pairs={{32,0},{64,32},{96,64},{128,96},{160,128},{192,160},{224,192},{33,... | collective-permute-start | bytes 491528 | tf_op jit(solution)/shard_map/ppermute | solution.py:28
  13.5 6.7 %collective-permute-start.2 = (f32[1,4,80,128]{3,1,2,0:T(4,128)}, f32[1,4,80,128]{3,1,2,0:T(4,128)}, u32[]{:S(2)}, u32[]{:S(2)}) collective-permute-start(f32[1,4,80,128]{3,1,2,0:T(4,128)} %bitcast.17), channel_id=1, source_target_pairs={{0,1},{1,2},{2,3},{3,4},{4,5},{5,6},{6,7},{7,8},{8,9},{9,10},{10,1... | collective-permute-start | bytes 491528 | tf_op jit(solution)/shard_map/ppermute | solution.py:26
  21.0 2.4 %collective-permute-start.3 = (f32[1,4,80,128]{3,1,2,0:T(4,128)}, f32[1,4,80,128]{3,1,2,0:T(4,128)}, u32[]{:S(2)}, u32[]{:S(2)}) collective-permute-start(f32[1,4,80,128]{3,1,2,0:T(4,128)} %bitcast.22), channel_id=1, source_target_pairs={{1,0},{2,1},{3,2},{4,3},{5,4},{6,5},{7,6},{8,7},{9,8},{10,9},{11,1... | collective-permute-start | bytes 491528 | tf_op jit(solution)/shard_map/ppermute | solution.py:28
  27.7 1.6 fusion.36
  29.2 2.3 %collective-permute-done.3 = f32[1,4,80,128]{3,1,2,0:T(4,128)} collective-permute-done((f32[1,4,80,128]{3,1,2,0:T(4,128)}, f32[1,4,80,128]{3,1,2,0:T(4,128)}, u32[]{:S(2)}, u32[]{:S(2)}) %collective-permute-start.3) | collective-permute-done | bytes 163872 | tf_op jit(solution)/shard_map/ppermute | solution.py:28
  34.7 1.6 convolution_bitcast_fusion.3
  36.3 2.0 %fusion.14 = f32[4,320,128]{2,1,0:T(8,128)S(1)} fusion(f32[4,320,128]{2,1,0:T(8,128)S(1)} %convolution_bitcast_fusion.3, f32[4,128,320]{1,2,0:T(8,128)S(1)} %convolution_multiply_fusion.3, f32[4,320,320]{2,1,0:T(8,128)S(1)} %copy-done, f32[4,320,128]{2,1,0:T(8,128)S(1)} %copy-done.2, f32[4]{0:T(128)S(1)} %compare_convert_fusion), kind=kOutput, calls=%fused_computation.26 | convolution fusion | flops 629637120 | bytes 4259856 | tf_op jit(solution)/shard_map/epq,eqr->epr/dot_general | solution.py:48
  38.3 2.0 %fusion.12 = f32[4,320,128]{2,1,0:T(8,128)S(1)} fusion(f32[4,320,128]{2,1,0:T(8,128)S(1)} %fusion.14, f32[4,320,320]{2,1,0:T(8,128)S(1)} %copy-done.1, f32[4,128,320]{1,2,0:T(8,128)S(1)} %convolution_multiply_fusion.3), kind=kOutput, calls=%fused_computation.23 | convolution fusion | flops 629473280 | bytes 3604480 | tf_op jit(solution)/shard_map/epq,eqr->epr/dot_general | solution.py:48
  40.5 1.9 %collective-permute-start.4 = (f32[1,4,80,128]{3,1,2,0:T(4,128)S(1)}, f32[1,4,80,128]{3,1,2,0:T(4,128)S(1)}, u32[]{:S(2)}, u32[]{:S(2)}) collective-permute-start(f32[1,4,80,128]{3,1,2,0:T(4,128)S(1)} %bitcast.555), channel_id=1, source_target_pairs={{0,32},{32,64},{64,96},{96,128},{128,160},{160,192},{192,224},{1,3... | collective-permute-start | bytes 491528 | tf_op jit(solution)/shard_map/ppermute | solution.py:26
  42.5 5.5 %collective-permute-start.5 = (f32[1,4,80,128]{3,1,2,0:T(4,128)S(1)}, f32[1,4,80,128]{3,1,2,0:T(4,128)S(1)}, u32[]{:S(2)}, u32[]{:S(2)}) collective-permute-start(f32[1,4,80,128]{3,1,2,0:T(4,128)S(1)} %bitcast.567), channel_id=1, source_target_pairs={{32,0},{64,32},{96,64},{128,96},{160,128},{192,160},{224,192},{33,... | collective-permute-start | bytes 491528 | tf_op jit(solution)/shard_map/ppermute | solution.py:28
  48.0 5.5 %collective-permute-start.6 = (f32[1,4,80,128]{3,1,2,0:T(4,128)S(1)}, f32[1,4,80,128]{3,1,2,0:T(4,128)S(1)}, u32[]{:S(2)}, u32[]{:S(2)}) collective-permute-start(f32[1,4,80,128]{3,1,2,0:T(4,128)S(1)} %bitcast.557), channel_id=1, source_target_pairs={{0,1},{1,2},{2,3},{3,4},{4,5},{5,6},{6,7},{7,8},{8,9},{9,10},{10,1... | collective-permute-start | bytes 491528 | tf_op jit(solution)/shard_map/ppermute | solution.py:26
  53.6 2.1 %collective-permute-start.7 = (f32[1,4,80,128]{3,1,2,0:T(4,128)S(1)}, f32[1,4,80,128]{3,1,2,0:T(4,128)S(1)}, u32[]{:S(2)}, u32[]{:S(2)}) collective-permute-start(f32[1,4,80,128]{3,1,2,0:T(4,128)S(1)} %bitcast.559), channel_id=1, source_target_pairs={{1,0},{2,1},{3,2},{4,3},{5,4},{6,5},{7,6},{8,7},{9,8},{10,9},{11,1... | collective-permute-start | bytes 491528 | tf_op jit(solution)/shard_map/ppermute | solution.py:28
  57.6 6.2 %collective-permute-done.7 = f32[1,4,80,128]{3,1,2,0:T(4,128)S(1)} collective-permute-done((f32[1,4,80,128]{3,1,2,0:T(4,128)S(1)}, f32[1,4,80,128]{3,1,2,0:T(4,128)S(1)}, u32[]{:S(2)}, u32[]{:S(2)}) %collective-permute-start.7) | collective-permute-done | bytes 163872 | tf_op jit(solution)/shard_map/ppermute | solution.py:28
  66.0 1.6 convolution_bitcast_fusion.2
  67.6 1.9 fusion.10
  70.5 1.9 %collective-permute-start.8 = (f32[1,4,20,128]{3,1,2,0:T(4,128)S(1)}, f32[1,4,20,128]{3,1,2,0:T(4,128)S(1)}, u32[]{:S(2)}, u32[]{:S(2)}) collective-permute-start(f32[1,4,20,128]{3,1,2,0:T(4,128)S(1)} %bitcast.583), channel_id=1, source_target_pairs={{0,32},{32,64},{64,96},{96,128},{128,160},{160,192},{192,224},{1,3... | collective-permute-start | bytes 122888 | tf_op jit(solution)/shard_map/ppermute | solution.py:26
  72.5 5.5 %collective-permute-start.9 = (f32[1,4,20,128]{3,1,2,0:T(4,128)S(1)}, f32[1,4,20,128]{3,1,2,0:T(4,128)S(1)}, u32[]{:S(2)}, u32[]{:S(2)}) collective-permute-start(f32[1,4,20,128]{3,1,2,0:T(4,128)S(1)} %bitcast.601), channel_id=1, source_target_pairs={{32,0},{64,32},{96,64},{128,96},{160,128},{192,160},{224,192},{33,... | collective-permute-start | bytes 122888 | tf_op jit(solution)/shard_map/ppermute | solution.py:28
  78.0 2.3 %collective-permute-start.10 = (f32[1,4,20,128]{3,1,2,0:T(4,128)S(1)}, f32[1,4,20,128]{3,1,2,0:T(4,128)S(1)}, u32[]{:S(2)}, u32[]{:S(2)}) collective-permute-start(f32[1,4,20,128]{3,1,2,0:T(4,128)S(1)} %bitcast.589), channel_id=1, source_target_pairs={{0,1},{1,2},{2,3},{3,4},{4,5},{5,6},{6,7},{7,8},{8,9},{9,10},{10,1... | collective-permute-start | bytes 122888 | tf_op jit(solution)/shard_map/ppermute | solution.py:26
  80.3 2.0 %collective-permute-start.11 = (f32[1,4,20,128]{3,1,2,0:T(4,128)S(1)}, f32[1,4,20,128]{3,1,2,0:T(4,128)S(1)}, u32[]{:S(2)}, u32[]{:S(2)}) collective-permute-start(f32[1,4,20,128]{3,1,2,0:T(4,128)S(1)} %bitcast.591), channel_id=1, source_target_pairs={{1,0},{2,1},{3,2},{4,3},{5,4},{6,5},{7,6},{8,7},{9,8},{10,9},{11,1... | collective-permute-start | bytes 122888 | tf_op jit(solution)/shard_map/ppermute | solution.py:28
  83.3 6.0 %collective-permute-done.11 = f32[1,4,20,128]{3,1,2,0:T(4,128)S(1)} collective-permute-done((f32[1,4,20,128]{3,1,2,0:T(4,128)S(1)}, f32[1,4,20,128]{3,1,2,0:T(4,128)S(1)}, u32[]{:S(2)}, u32[]{:S(2)}) %collective-permute-start.11) | collective-permute-done | bytes 40992 | tf_op jit(solution)/shard_map/ppermute | solution.py:28
  91.3 1.9 %collective-permute-start.12 = (f32[1,4,20,128]{3,1,2,0:T(4,128)S(1)}, f32[1,4,20,128]{3,1,2,0:T(4,128)S(1)}, u32[]{:S(2)}, u32[]{:S(2)}) collective-permute-start(f32[1,4,20,128]{3,1,2,0:T(4,128)S(1)} %bitcast.585), channel_id=1, source_target_pairs={{0,32},{32,64},{64,96},{96,128},{128,160},{160,192},{192,224},{1,3... | collective-permute-start | bytes 122888 | tf_op jit(solution)/shard_map/ppermute | solution.py:26
  93.3 5.5 %collective-permute-start.13 = (f32[1,4,20,128]{3,1,2,0:T(4,128)S(1)}, f32[1,4,20,128]{3,1,2,0:T(4,128)S(1)}, u32[]{:S(2)}, u32[]{:S(2)}) collective-permute-start(f32[1,4,20,128]{3,1,2,0:T(4,128)S(1)} %bitcast.603), channel_id=1, source_target_pairs={{32,0},{64,32},{96,64},{128,96},{160,128},{192,160},{224,192},{33,... | collective-permute-start | bytes 122888 | tf_op jit(solution)/shard_map/ppermute | solution.py:28
  98.8 2.5 %collective-permute-start.14 = (f32[1,4,20,128]{3,1,2,0:T(4,128)S(1)}, f32[1,4,20,128]{3,1,2,0:T(4,128)S(1)}, u32[]{:S(2)}, u32[]{:S(2)}) collective-permute-start(f32[1,4,20,128]{3,1,2,0:T(4,128)S(1)} %bitcast.593), channel_id=1, source_target_pairs={{0,1},{1,2},{2,3},{3,4},{4,5},{5,6},{6,7},{7,8},{8,9},{9,10},{10,1... | collective-permute-start | bytes 122888 | tf_op jit(solution)/shard_map/ppermute | solution.py:26
  101.3 1.9 %collective-permute-start.15 = (f32[1,4,20,128]{3,1,2,0:T(4,128)S(1)}, f32[1,4,20,128]{3,1,2,0:T(4,128)S(1)}, u32[]{:S(2)}, u32[]{:S(2)}) collective-permute-start(f32[1,4,20,128]{3,1,2,0:T(4,128)S(1)} %bitcast.595), channel_id=1, source_target_pairs={{1,0},{2,1},{3,2},{4,3},{5,4},{6,5},{7,6},{8,7},{9,8},{10,9},{11,1... | collective-permute-start | bytes 122888 | tf_op jit(solution)/shard_map/ppermute | solution.py:28
  104.2 6.1 %collective-permute-done.15 = f32[1,4,20,128]{3,1,2,0:T(4,128)S(1)} collective-permute-done((f32[1,4,20,128]{3,1,2,0:T(4,128)S(1)}, f32[1,4,20,128]{3,1,2,0:T(4,128)S(1)}, u32[]{:S(2)}, u32[]{:S(2)}) %collective-permute-start.15) | collective-permute-done | bytes 40992 | tf_op jit(solution)/shard_map/ppermute | solution.py:28
  112.4 1.9 %collective-permute-start.16 = (f32[1,4,20,128]{3,1,2,0:T(4,128)S(1)}, f32[1,4,20,128]{3,1,2,0:T(4,128)S(1)}, u32[]{:S(2)}, u32[]{:S(2)}) collective-permute-start(f32[1,4,20,128]{3,1,2,0:T(4,128)S(1)} %bitcast.587), channel_id=1, source_target_pairs={{0,32},{32,64},{64,96},{96,128},{128,160},{160,192},{192,224},{1,3... | collective-permute-start | bytes 122888 | tf_op jit(solution)/shard_map/ppermute | solution.py:26
  114.4 5.5 %collective-permute-start.17 = (f32[1,4,20,128]{3,1,2,0:T(4,128)S(1)}, f32[1,4,20,128]{3,1,2,0:T(4,128)S(1)}, u32[]{:S(2)}, u32[]{:S(2)}) collective-permute-start(f32[1,4,20,128]{3,1,2,0:T(4,128)S(1)} %bitcast.605), channel_id=1, source_target_pairs={{32,0},{64,32},{96,64},{128,96},{160,128},{192,160},{224,192},{33,... | collective-permute-start | bytes 122888 | tf_op jit(solution)/shard_map/ppermute | solution.py:28
  119.9 2.5 %collective-permute-start.18 = (f32[1,4,20,128]{3,1,2,0:T(4,128)S(1)}, f32[1,4,20,128]{3,1,2,0:T(4,128)S(1)}, u32[]{:S(2)}, u32[]{:S(2)}) collective-permute-start(f32[1,4,20,128]{3,1,2,0:T(4,128)S(1)} %bitcast.597), channel_id=1, source_target_pairs={{0,1},{1,2},{2,3},{3,4},{4,5},{5,6},{6,7},{7,8},{8,9},{9,10},{10,1... | collective-permute-start | bytes 122888 | tf_op jit(solution)/shard_map/ppermute | solution.py:26
  122.3 2.1 %collective-permute-start.19 = (f32[1,4,20,128]{3,1,2,0:T(4,128)S(1)}, f32[1,4,20,128]{3,1,2,0:T(4,128)S(1)}, u32[]{:S(2)}, u32[]{:S(2)}) collective-permute-start(f32[1,4,20,128]{3,1,2,0:T(4,128)S(1)} %bitcast.599), channel_id=1, source_target_pairs={{1,0},{2,1},{3,2},{4,3},{5,4},{6,5},{7,6},{8,7},{9,8},{10,9},{11,1... | collective-permute-start | bytes 122888 | tf_op jit(solution)/shard_map/ppermute | solution.py:28
  125.4 5.9 %collective-permute-done.19 = f32[1,4,20,128]{3,1,2,0:T(4,128)S(1)} collective-permute-done((f32[1,4,20,128]{3,1,2,0:T(4,128)S(1)}, f32[1,4,20,128]{3,1,2,0:T(4,128)S(1)}, u32[]{:S(2)}, u32[]{:S(2)}) %collective-permute-start.19) | collective-permute-done | bytes 40992 | tf_op jit(solution)/shard_map/ppermute | solution.py:28
  134.2 1.9 %collective-permute-start.20 = (f32[1,4,80,128]{3,1,2,0:T(4,128)S(1)}, f32[1,4,80,128]{3,1,2,0:T(4,128)S(1)}, u32[]{:S(2)}, u32[]{:S(2)}) collective-permute-start(f32[1,4,80,128]{3,1,2,0:T(4,128)S(1)} %bitcast.561), channel_id=1, source_target_pairs={{0,32},{32,64},{64,96},{96,128},{128,160},{160,192},{192,224},{1,3... | collective-permute-start | bytes 491528 | tf_op jit(solution)/shard_map/ppermute | solution.py:26
  136.2 5.5 %collective-permute-start.21 = (f32[1,4,80,128]{3,1,2,0:T(4,128)S(1)}, f32[1,4,80,128]{3,1,2,0:T(4,128)S(1)}, u32[]{:S(2)}, u32[]{:S(2)}) collective-permute-start(f32[1,4,80,128]{3,1,2,0:T(4,128)S(1)} %bitcast.569), channel_id=1, source_target_pairs={{32,0},{64,32},{96,64},{128,96},{160,128},{192,160},{224,192},{33,... | collective-permute-start | bytes 491528 | tf_op jit(solution)/shard_map/ppermute | solution.py:28
  141.7 2.5 %collective-permute-start.22 = (f32[1,4,80,128]{3,1,2,0:T(4,128)S(1)}, f32[1,4,80,128]{3,1,2,0:T(4,128)S(1)}, u32[]{:S(2)}, u32[]{:S(2)}) collective-permute-start(f32[1,4,80,128]{3,1,2,0:T(4,128)S(1)} %bitcast.563), channel_id=1, source_target_pairs={{0,1},{1,2},{2,3},{3,4},{4,5},{5,6},{6,7},{7,8},{8,9},{9,10},{10,1... | collective-permute-start | bytes 491528 | tf_op jit(solution)/shard_map/ppermute | solution.py:26
  144.3 1.9 %collective-permute-start.23 = (f32[1,4,80,128]{3,1,2,0:T(4,128)S(1)}, f32[1,4,80,128]{3,1,2,0:T(4,128)S(1)}, u32[]{:S(2)}, u32[]{:S(2)}) collective-permute-start(f32[1,4,80,128]{3,1,2,0:T(4,128)S(1)} %bitcast.565), channel_id=1, source_target_pairs={{1,0},{2,1},{3,2},{4,3},{5,4},{6,5},{7,6},{8,7},{9,8},{10,9},{11,1... | collective-permute-start | bytes 491528 | tf_op jit(solution)/shard_map/ppermute | solution.py:28
  148.1 6.4 %collective-permute-done.23 = f32[1,4,80,128]{3,1,2,0:T(4,128)S(1)} collective-permute-done((f32[1,4,80,128]{3,1,2,0:T(4,128)S(1)}, f32[1,4,80,128]{3,1,2,0:T(4,128)S(1)}, u32[]{:S(2)}, u32[]{:S(2)}) %collective-permute-start.23) | collective-permute-done | bytes 163872 | tf_op jit(solution)/shard_map/ppermute | solution.py:28
  156.7 1.6 convolution_bitcast_fusion.1
  158.2 1.9 fusion.7
  160.1 2.0 %fusion.5 = f32[4,320,128]{2,1,0:T(8,128)S(1)} fusion(f32[4,320,128]{2,1,0:T(8,128)S(1)} %fusion.8, f32[4,320,128]{2,1,0:T(8,128)S(1)} %fusion.7, f32[4,320,320]{2,1,0:T(8,128)S(1)} %copy-done.1), kind=kOutput, calls=%fused_computation.12 | convolution fusion | flops 629473280 | bytes 3604480 | tf_op jit(solution)/shard_map/epq,eqr->epr/dot_general | solution.py:48
  162.3 1.9 %collective-permute-start.24 = (f32[1,4,80,128]{3,1,2,0:T(4,128)S(1)}, f32[1,4,80,128]{3,1,2,0:T(4,128)S(1)}, u32[]{:S(2)}, u32[]{:S(2)}) collective-permute-start(f32[1,4,80,128]{3,1,2,0:T(4,128)S(1)} %bitcast.553), channel_id=1, source_target_pairs={{0,32},{32,64},{64,96},{96,128},{128,160},{160,192},{192,224},{1,3... | collective-permute-start | bytes 491528 | tf_op jit(solution)/shard_map/ppermute | solution.py:26
  164.3 5.5 %collective-permute-start.25 = (f32[1,4,80,128]{3,1,2,0:T(4,128)S(1)}, f32[1,4,80,128]{3,1,2,0:T(4,128)S(1)}, u32[]{:S(2)}, u32[]{:S(2)}) collective-permute-start(f32[1,4,80,128]{3,1,2,0:T(4,128)S(1)} %bitcast.551), channel_id=1, source_target_pairs={{32,0},{64,32},{96,64},{128,96},{160,128},{192,160},{224,192},{33,... | collective-permute-start | bytes 491528 | tf_op jit(solution)/shard_map/ppermute | solution.py:28
  169.9 2.6 %collective-permute-start.26 = (f32[1,4,80,128]{3,1,2,0:T(4,128)S(1)}, f32[1,4,80,128]{3,1,2,0:T(4,128)S(1)}, u32[]{:S(2)}, u32[]{:S(2)}) collective-permute-start(f32[1,4,80,128]{3,1,2,0:T(4,128)S(1)} %bitcast.549), channel_id=1, source_target_pairs={{0,1},{1,2},{2,3},{3,4},{4,5},{5,6},{6,7},{7,8},{8,9},{9,10},{10,1... | collective-permute-start | bytes 491528 | tf_op jit(solution)/shard_map/ppermute | solution.py:26
  172.5 2.0 %collective-permute-start.27 = (f32[1,4,80,128]{3,1,2,0:T(4,128)S(1)}, f32[1,4,80,128]{3,1,2,0:T(4,128)S(1)}, u32[]{:S(2)}, u32[]{:S(2)}) collective-permute-start(f32[1,4,80,128]{3,1,2,0:T(4,128)S(1)} %bitcast.547), channel_id=1, source_target_pairs={{1,0},{2,1},{3,2},{4,3},{5,4},{6,5},{7,6},{8,7},{9,8},{10,9},{11,1... | collective-permute-start | bytes 491528 | tf_op jit(solution)/shard_map/ppermute | solution.py:28
  176.4 6.3 %collective-permute-done.27 = f32[1,4,80,128]{3,1,2,0:T(4,128)S(1)} collective-permute-done((f32[1,4,80,128]{3,1,2,0:T(4,128)S(1)}, f32[1,4,80,128]{3,1,2,0:T(4,128)S(1)}, u32[]{:S(2)}, u32[]{:S(2)}) %collective-permute-start.27) | collective-permute-done | bytes 163872 | tf_op jit(solution)/shard_map/ppermute | solution.py:28
  184.9 1.6 convolution_bitcast_fusion
  186.5 2.0 %fusion.3 = f32[4,320,128]{2,1,0:T(8,128)S(1)} fusion(f32[4,320,128]{2,1,0:T(8,128)S(1)} %convolution_bitcast_fusion, f32[4,320,128]{2,1,0:T(8,128)S(1)} %fusion.5, f32[4,320,320]{2,1,0:T(8,128)S(1)} %copy-done, f32[4,320,128]{2,1,0:T(8,128)S(1)} %copy-done.2, f32[4]{0:T(128)S(1)} %compare_convert_fusion), kind=kOutput, calls=%fused_computation.9 | convolution fusion | flops 629637120 | bytes 4259856 | tf_op jit(solution)/shard_map/epq,eqr->epr/dot_general | solution.py:48
  188.4 2.7 %fusion.1 = f32[4,320,128]{2,1,0:T(8,128)} fusion(f32[4,320,128]{2,1,0:T(8,128)S(1)} %fusion.5, f32[4,320,128]{2,1,0:T(8,128)S(1)} %fusion.3, f32[4,320,320]{2,1,0:T(8,128)S(1)} %copy-done.1), kind=kOutput, calls=%fused_computation.6 | convolution fusion | flops 629473280 | bytes 3604480 | tf_op jit(solution)/shard_map/epq,eqr->epr/dot_general | solution.py:48
  (173 shorter events, 33.1 us)
Async XLA Ops:
  0.0 36.3 %copy-start = (f32[4,320,320]{2,1,0:T(8,128)S(1)}, f32[4,320,320]{2,1,0:T(8,128)}, u32[]{:S(2)}) copy-start(f32[4,320,320]{2,1,0:T(8,128)} %param.13) | copy-start | bytes 4915204
  4.5 19.2 %copy-start.10 = (s32[4,6]{1,0:T(4,128)S(1)}, s32[4,6]{1,0:T(4,128)}, u32[]{:S(2)}) copy-start(s32[4,6]{1,0:T(4,128)} %param.21) | copy-start | bytes 292
  4.5 19.7 %copy-start.8 = (f32[4,6,80]{2,0,1:T(4,128)S(1)}, f32[4,6,80]{2,0,1:T(4,128)}, u32[]{:S(2)}) copy-start(f32[4,6,80]{2,0,1:T(4,128)} %param.16) | copy-start | bytes 23044
  4.5 19.8 %copy-start.9 = (f32[4,6,20]{2,0,1:T(4,128)S(1)}, f32[4,6,20]{2,0,1:T(4,128)}, u32[]{:S(2)}) copy-start(f32[4,6,20]{2,0,1:T(4,128)} %param.20) | copy-start | bytes 5764
  4.6 20.1 %collective-permute-start = (f32[1,4,80,128]{3,1,2,0:T(4,128)S(1)}, f32[1,4,80,128]{3,1,2,0:T(4,128)}, u32[]{:S(2)}, u32[]{:S(2)}) collective-permute-start(f32[1,4,80,128]{3,1,2,0:T(4,128)S(1)} %bitcast.545), channel_id=1, source_target_pairs={{0,32},{32,64},{64,96},{96,128},{128,160},{160,192},{192,224},{1,3... | collective-permute-start | bytes 491528 | tf_op jit(solution)/shard_map/ppermute | solution.py:26
  8.6 17.6 %collective-permute-start.1 = (f32[1,4,80,128]{3,1,2,0:T(4,128)}, f32[1,4,80,128]{3,1,2,0:T(4,128)}, u32[]{:S(2)}, u32[]{:S(2)}) collective-permute-start(f32[1,4,80,128]{3,1,2,0:T(4,128)} %bitcast.12), channel_id=1, source_target_pairs={{32,0},{64,32},{96,64},{128,96},{160,128},{192,160},{224,192},{33,... | collective-permute-start | bytes 491528 | tf_op jit(solution)/shard_map/ppermute | solution.py:28
  13.5 14.1 %collective-permute-start.2 = (f32[1,4,80,128]{3,1,2,0:T(4,128)}, f32[1,4,80,128]{3,1,2,0:T(4,128)}, u32[]{:S(2)}, u32[]{:S(2)}) collective-permute-start(f32[1,4,80,128]{3,1,2,0:T(4,128)} %bitcast.17), channel_id=1, source_target_pairs={{0,1},{1,2},{2,3},{3,4},{4,5},{5,6},{6,7},{7,8},{8,9},{9,10},{10,1... | collective-permute-start | bytes 491528 | tf_op jit(solution)/shard_map/ppermute | solution.py:26
  21.0 10.6 %collective-permute-start.3 = (f32[1,4,80,128]{3,1,2,0:T(4,128)}, f32[1,4,80,128]{3,1,2,0:T(4,128)}, u32[]{:S(2)}, u32[]{:S(2)}) collective-permute-start(f32[1,4,80,128]{3,1,2,0:T(4,128)} %bitcast.22), channel_id=1, source_target_pairs={{1,0},{2,1},{3,2},{4,3},{5,4},{6,5},{7,6},{8,7},{9,8},{10,9},{11,1... | collective-permute-start | bytes 491528 | tf_op jit(solution)/shard_map/ppermute | solution.py:28
  27.6 7.1 %copy-start.3 = (f32[6,320,80]{1,2,0:T(8,128)S(1)}, f32[6,320,80]{1,2,0:T(8,128)}, u32[]{:S(2)}) copy-start(f32[6,320,80]{1,2,0:T(8,128)} %param.15) | copy-start | bytes 1843204
  34.1 2.2 %copy-start.2 = (f32[4,320,128]{2,1,0:T(8,128)S(1)}, f32[4,320,128]{2,1,0:T(8,128)}, u32[]{:S(2)}) copy-start(f32[4,320,128]{2,1,0:T(8,128)} %param.12) | copy-start | bytes 1966084
  36.3 2.0 %copy-start.1 = (f32[4,320,320]{2,1,0:T(8,128)S(1)}, f32[4,320,320]{2,1,0:T(8,128)}, u32[]{:S(2)}) copy-start(f32[4,320,320]{2,1,0:T(8,128)} %param.14) | copy-start | bytes 4915204
  40.5 15.6 %collective-permute-start.4 = (f32[1,4,80,128]{3,1,2,0:T(4,128)S(1)}, f32[1,4,80,128]{3,1,2,0:T(4,128)S(1)}, u32[]{:S(2)}, u32[]{:S(2)}) collective-permute-start(f32[1,4,80,128]{3,1,2,0:T(4,128)S(1)} %bitcast.555), channel_id=1, source_target_pairs={{0,32},{32,64},{64,96},{96,128},{128,160},{160,192},{192,224},{1,3... | collective-permute-start | bytes 491528 | tf_op jit(solution)/shard_map/ppermute | solution.py:26
  42.5 14.1 %collective-permute-start.5 = (f32[1,4,80,128]{3,1,2,0:T(4,128)S(1)}, f32[1,4,80,128]{3,1,2,0:T(4,128)S(1)}, u32[]{:S(2)}, u32[]{:S(2)}) collective-permute-start(f32[1,4,80,128]{3,1,2,0:T(4,128)S(1)} %bitcast.567), channel_id=1, source_target_pairs={{32,0},{64,32},{96,64},{128,96},{160,128},{192,160},{224,192},{33,... | collective-permute-start | bytes 491528 | tf_op jit(solution)/shard_map/ppermute | solution.py:28
  48.0 9.1 %collective-permute-start.6 = (f32[1,4,80,128]{3,1,2,0:T(4,128)S(1)}, f32[1,4,80,128]{3,1,2,0:T(4,128)S(1)}, u32[]{:S(2)}, u32[]{:S(2)}) collective-permute-start(f32[1,4,80,128]{3,1,2,0:T(4,128)S(1)} %bitcast.557), channel_id=1, source_target_pairs={{0,1},{1,2},{2,3},{3,4},{4,5},{5,6},{6,7},{7,8},{8,9},{9,10},{10,1... | collective-permute-start | bytes 491528 | tf_op jit(solution)/shard_map/ppermute | solution.py:26
  53.6 10.3 %collective-permute-start.7 = (f32[1,4,80,128]{3,1,2,0:T(4,128)S(1)}, f32[1,4,80,128]{3,1,2,0:T(4,128)S(1)}, u32[]{:S(2)}, u32[]{:S(2)}) collective-permute-start(f32[1,4,80,128]{3,1,2,0:T(4,128)S(1)} %bitcast.559), channel_id=1, source_target_pairs={{1,0},{2,1},{3,2},{4,3},{5,4},{6,5},{7,6},{8,7},{9,8},{10,9},{11,1... | collective-permute-start | bytes 491528 | tf_op jit(solution)/shard_map/ppermute | solution.py:28
  67.6 1.9 copy-start.7
  67.6 2.5 %copy-start.4 = (f32[4,40,40]{2,1,0:T(8,128)S(1)}, f32[4,40,40]{2,1,0:T(8,128)}, u32[]{:S(2)}) copy-start(f32[4,40,40]{2,1,0:T(8,128)} %param.18) | copy-start | bytes 76804
  69.5 20.8 %copy-start.6 = (f32[6,40,20]{1,2,0:T(8,128)S(1)}, f32[6,40,20]{1,2,0:T(8,128)}, u32[]{:S(2)}) copy-start(f32[6,40,20]{1,2,0:T(8,128)} %param.19) | copy-start | bytes 57604
  69.5 21.1 %copy-start.5 = (f32[4,40,40]{2,1,0:T(8,128)S(1)}, f32[4,40,40]{2,1,0:T(8,128)}, u32[]{:S(2)}) copy-start(f32[4,40,40]{2,1,0:T(8,128)} %param.17) | copy-start | bytes 76804
  70.5 11.9 %collective-permute-start.8 = (f32[1,4,20,128]{3,1,2,0:T(4,128)S(1)}, f32[1,4,20,128]{3,1,2,0:T(4,128)S(1)}, u32[]{:S(2)}, u32[]{:S(2)}) collective-permute-start(f32[1,4,20,128]{3,1,2,0:T(4,128)S(1)} %bitcast.583), channel_id=1, source_target_pairs={{0,32},{32,64},{64,96},{96,128},{128,160},{160,192},{192,224},{1,3... | collective-permute-start | bytes 122888 | tf_op jit(solution)/shard_map/ppermute | solution.py:26
  72.5 10.2 %collective-permute-start.9 = (f32[1,4,20,128]{3,1,2,0:T(4,128)S(1)}, f32[1,4,20,128]{3,1,2,0:T(4,128)S(1)}, u32[]{:S(2)}, u32[]{:S(2)}) collective-permute-start(f32[1,4,20,128]{3,1,2,0:T(4,128)S(1)} %bitcast.601), channel_id=1, source_target_pairs={{32,0},{64,32},{96,64},{128,96},{160,128},{192,160},{224,192},{33,... | collective-permute-start | bytes 122888 | tf_op jit(solution)/shard_map/ppermute | solution.py:28
  78.0 5.0 %collective-permute-start.10 = (f32[1,4,20,128]{3,1,2,0:T(4,128)S(1)}, f32[1,4,20,128]{3,1,2,0:T(4,128)S(1)}, u32[]{:S(2)}, u32[]{:S(2)}) collective-permute-start(f32[1,4,20,128]{3,1,2,0:T(4,128)S(1)} %bitcast.589), channel_id=1, source_target_pairs={{0,1},{1,2},{2,3},{3,4},{4,5},{5,6},{6,7},{7,8},{8,9},{9,10},{10,1... | collective-permute-start | bytes 122888 | tf_op jit(solution)/shard_map/ppermute | solution.py:26
  80.3 8.9 %collective-permute-start.11 = (f32[1,4,20,128]{3,1,2,0:T(4,128)S(1)}, f32[1,4,20,128]{3,1,2,0:T(4,128)S(1)}, u32[]{:S(2)}, u32[]{:S(2)}) collective-permute-start(f32[1,4,20,128]{3,1,2,0:T(4,128)S(1)} %bitcast.591), channel_id=1, source_target_pairs={{1,0},{2,1},{3,2},{4,3},{5,4},{6,5},{7,6},{8,7},{9,8},{10,9},{11,1... | collective-permute-start | bytes 122888 | tf_op jit(solution)/shard_map/ppermute | solution.py:28
  91.3 11.9 %collective-permute-start.12 = (f32[1,4,20,128]{3,1,2,0:T(4,128)S(1)}, f32[1,4,20,128]{3,1,2,0:T(4,128)S(1)}, u32[]{:S(2)}, u32[]{:S(2)}) collective-permute-start(f32[1,4,20,128]{3,1,2,0:T(4,128)S(1)} %bitcast.585), channel_id=1, source_target_pairs={{0,32},{32,64},{64,96},{96,128},{128,160},{160,192},{192,224},{1,3... | collective-permute-start | bytes 122888 | tf_op jit(solution)/shard_map/ppermute | solution.py:26
  93.3 10.2 %collective-permute-start.13 = (f32[1,4,20,128]{3,1,2,0:T(4,128)S(1)}, f32[1,4,20,128]{3,1,2,0:T(4,128)S(1)}, u32[]{:S(2)}, u32[]{:S(2)}) collective-permute-start(f32[1,4,20,128]{3,1,2,0:T(4,128)S(1)} %bitcast.603), channel_id=1, source_target_pairs={{32,0},{64,32},{96,64},{128,96},{160,128},{192,160},{224,192},{33,... | collective-permute-start | bytes 122888 | tf_op jit(solution)/shard_map/ppermute | solution.py:28
  98.8 5.0 %collective-permute-start.14 = (f32[1,4,20,128]{3,1,2,0:T(4,128)S(1)}, f32[1,4,20,128]{3,1,2,0:T(4,128)S(1)}, u32[]{:S(2)}, u32[]{:S(2)}) collective-permute-start(f32[1,4,20,128]{3,1,2,0:T(4,128)S(1)} %bitcast.593), channel_id=1, source_target_pairs={{0,1},{1,2},{2,3},{3,4},{4,5},{5,6},{6,7},{7,8},{8,9},{9,10},{10,1... | collective-permute-start | bytes 122888 | tf_op jit(solution)/shard_map/ppermute | solution.py:26
  101.3 8.9 %collective-permute-start.15 = (f32[1,4,20,128]{3,1,2,0:T(4,128)S(1)}, f32[1,4,20,128]{3,1,2,0:T(4,128)S(1)}, u32[]{:S(2)}, u32[]{:S(2)}) collective-permute-start(f32[1,4,20,128]{3,1,2,0:T(4,128)S(1)} %bitcast.595), channel_id=1, source_target_pairs={{1,0},{2,1},{3,2},{4,3},{5,4},{6,5},{7,6},{8,7},{9,8},{10,9},{11,1... | collective-permute-start | bytes 122888 | tf_op jit(solution)/shard_map/ppermute | solution.py:28
  112.4 12.2 %collective-permute-start.16 = (f32[1,4,20,128]{3,1,2,0:T(4,128)S(1)}, f32[1,4,20,128]{3,1,2,0:T(4,128)S(1)}, u32[]{:S(2)}, u32[]{:S(2)}) collective-permute-start(f32[1,4,20,128]{3,1,2,0:T(4,128)S(1)} %bitcast.587), channel_id=1, source_target_pairs={{0,32},{32,64},{64,96},{96,128},{128,160},{160,192},{192,224},{1,3... | collective-permute-start | bytes 122888 | tf_op jit(solution)/shard_map/ppermute | solution.py:26
  114.4 10.5 %collective-permute-start.17 = (f32[1,4,20,128]{3,1,2,0:T(4,128)S(1)}, f32[1,4,20,128]{3,1,2,0:T(4,128)S(1)}, u32[]{:S(2)}, u32[]{:S(2)}) collective-permute-start(f32[1,4,20,128]{3,1,2,0:T(4,128)S(1)} %bitcast.605), channel_id=1, source_target_pairs={{32,0},{64,32},{96,64},{128,96},{160,128},{192,160},{224,192},{33,... | collective-permute-start | bytes 122888 | tf_op jit(solution)/shard_map/ppermute | solution.py:28
  119.9 5.3 %collective-permute-start.18 = (f32[1,4,20,128]{3,1,2,0:T(4,128)S(1)}, f32[1,4,20,128]{3,1,2,0:T(4,128)S(1)}, u32[]{:S(2)}, u32[]{:S(2)}) collective-permute-start(f32[1,4,20,128]{3,1,2,0:T(4,128)S(1)} %bitcast.597), channel_id=1, source_target_pairs={{0,1},{1,2},{2,3},{3,4},{4,5},{5,6},{6,7},{7,8},{8,9},{9,10},{10,1... | collective-permute-start | bytes 122888 | tf_op jit(solution)/shard_map/ppermute | solution.py:26
  122.3 8.9 %collective-permute-start.19 = (f32[1,4,20,128]{3,1,2,0:T(4,128)S(1)}, f32[1,4,20,128]{3,1,2,0:T(4,128)S(1)}, u32[]{:S(2)}, u32[]{:S(2)}) collective-permute-start(f32[1,4,20,128]{3,1,2,0:T(4,128)S(1)} %bitcast.599), channel_id=1, source_target_pairs={{1,0},{2,1},{3,2},{4,3},{5,4},{6,5},{7,6},{8,7},{9,8},{10,9},{11,1... | collective-permute-start | bytes 122888 | tf_op jit(solution)/shard_map/ppermute | solution.py:28
  134.2 12.4 %collective-permute-start.20 = (f32[1,4,80,128]{3,1,2,0:T(4,128)S(1)}, f32[1,4,80,128]{3,1,2,0:T(4,128)S(1)}, u32[]{:S(2)}, u32[]{:S(2)}) collective-permute-start(f32[1,4,80,128]{3,1,2,0:T(4,128)S(1)} %bitcast.561), channel_id=1, source_target_pairs={{0,32},{32,64},{64,96},{96,128},{128,160},{160,192},{192,224},{1,3... | collective-permute-start | bytes 491528 | tf_op jit(solution)/shard_map/ppermute | solution.py:26
  136.2 10.9 %collective-permute-start.21 = (f32[1,4,80,128]{3,1,2,0:T(4,128)S(1)}, f32[1,4,80,128]{3,1,2,0:T(4,128)S(1)}, u32[]{:S(2)}, u32[]{:S(2)}) collective-permute-start(f32[1,4,80,128]{3,1,2,0:T(4,128)S(1)} %bitcast.569), channel_id=1, source_target_pairs={{32,0},{64,32},{96,64},{128,96},{160,128},{192,160},{224,192},{33,... | collective-permute-start | bytes 491528 | tf_op jit(solution)/shard_map/ppermute | solution.py:28
  141.7 5.9 %collective-permute-start.22 = (f32[1,4,80,128]{3,1,2,0:T(4,128)S(1)}, f32[1,4,80,128]{3,1,2,0:T(4,128)S(1)}, u32[]{:S(2)}, u32[]{:S(2)}) collective-permute-start(f32[1,4,80,128]{3,1,2,0:T(4,128)S(1)} %bitcast.563), channel_id=1, source_target_pairs={{0,1},{1,2},{2,3},{3,4},{4,5},{5,6},{6,7},{7,8},{8,9},{9,10},{10,1... | collective-permute-start | bytes 491528 | tf_op jit(solution)/shard_map/ppermute | solution.py:26
  144.3 10.3 %collective-permute-start.23 = (f32[1,4,80,128]{3,1,2,0:T(4,128)S(1)}, f32[1,4,80,128]{3,1,2,0:T(4,128)S(1)}, u32[]{:S(2)}, u32[]{:S(2)}) collective-permute-start(f32[1,4,80,128]{3,1,2,0:T(4,128)S(1)} %bitcast.565), channel_id=1, source_target_pairs={{1,0},{2,1},{3,2},{4,3},{5,4},{6,5},{7,6},{8,7},{9,8},{10,9},{11,1... | collective-permute-start | bytes 491528 | tf_op jit(solution)/shard_map/ppermute | solution.py:28
  162.3 12.6 %collective-permute-start.24 = (f32[1,4,80,128]{3,1,2,0:T(4,128)S(1)}, f32[1,4,80,128]{3,1,2,0:T(4,128)S(1)}, u32[]{:S(2)}, u32[]{:S(2)}) collective-permute-start(f32[1,4,80,128]{3,1,2,0:T(4,128)S(1)} %bitcast.553), channel_id=1, source_target_pairs={{0,32},{32,64},{64,96},{96,128},{128,160},{160,192},{192,224},{1,3... | collective-permute-start | bytes 491528 | tf_op jit(solution)/shard_map/ppermute | solution.py:26
  164.3 11.1 %collective-permute-start.25 = (f32[1,4,80,128]{3,1,2,0:T(4,128)S(1)}, f32[1,4,80,128]{3,1,2,0:T(4,128)S(1)}, u32[]{:S(2)}, u32[]{:S(2)}) collective-permute-start(f32[1,4,80,128]{3,1,2,0:T(4,128)S(1)} %bitcast.551), channel_id=1, source_target_pairs={{32,0},{64,32},{96,64},{128,96},{160,128},{192,160},{224,192},{33,... | collective-permute-start | bytes 491528 | tf_op jit(solution)/shard_map/ppermute | solution.py:28
  169.9 6.1 %collective-permute-start.26 = (f32[1,4,80,128]{3,1,2,0:T(4,128)S(1)}, f32[1,4,80,128]{3,1,2,0:T(4,128)S(1)}, u32[]{:S(2)}, u32[]{:S(2)}) collective-permute-start(f32[1,4,80,128]{3,1,2,0:T(4,128)S(1)} %bitcast.549), channel_id=1, source_target_pairs={{0,1},{1,2},{2,3},{3,4},{4,5},{5,6},{6,7},{7,8},{8,9},{9,10},{10,1... | collective-permute-start | bytes 491528 | tf_op jit(solution)/shard_map/ppermute | solution.py:26
  172.5 10.3 %collective-permute-start.27 = (f32[1,4,80,128]{3,1,2,0:T(4,128)S(1)}, f32[1,4,80,128]{3,1,2,0:T(4,128)S(1)}, u32[]{:S(2)}, u32[]{:S(2)}) collective-permute-start(f32[1,4,80,128]{3,1,2,0:T(4,128)S(1)} %bitcast.547), channel_id=1, source_target_pairs={{1,0},{2,1},{3,2},{4,3},{5,4},{6,5},{7,6},{8,7},{9,8},{10,9},{11,1... | collective-permute-start | bytes 491528 | tf_op jit(solution)/shard_map/ppermute | solution.py:28
where the time goes:
time: 195 us; the launch traced here: 191 us
  starting transfers between devices  90.7 us (47%)
  matrix products  49.6 us (25%)
  waiting for transfers between devices  39.2 us (20%)
  local copies, waits for them, and re-layouts  6.34 us (3%)
  other arithmetic  2.99 us (2%)
  between operations  2.59 us (1%)
    ppermute x14, starting transfers between devices, with_halo(): lax.ppermute(head, axis, [((i + 1) % count, i) for i in range(ends)])  51.6 us
    ppermute x14, starting transfers between devices, with_halo(): lax.ppermute(tail, axis, [(i, (i + 1) % count) for i in range(ends)])  39.2 us
    ppermute x14, waiting for transfers between devices, with_halo(): lax.ppermute(head, axis, [((i + 1) % count, i) for i in range(ends)])  39.1 us
    dot_general x42, matrix products, pick_rows(): return jnp.einsum('ab,bqr->aqr', selector, candidates, precision=highest)  21 us
    dot_general x15, matrix products, block_apply(): return jnp.einsum('epq,eqr->epr', blocks, vectors, precision=highest)  20 us
    dot_general x7, matrix products, lift_apply(): jnp.einsum('fpq,efqr->epr', face_lifts, face_coefs[:, :, :, None] * nearb...  7.36 us
  transfers between devices with their start and end apart: 28, of which 7 were waited for; matrix products, arithmetic and copies ran while one was open for 9% of the time, Pallas kernels for 0%

commit v1 on v0

v1 whole, which is shorter than its diff:
```python
import jax
import jax.numpy as jnp
import numpy as np
from jax import lax
from jax.experimental import pallas as pl
from jax.experimental.pallas import tpu as pltpu
from jax.sharding import PartitionSpec as P

NVAR = 5
SLOTS = 4
NF = 320
NFACE = 80
NC = 40
NCF = 20
HALO = 24
RHS = 128
WIDE = 8
NARROW = 32
MESH = pl.DeviceIdType.MESH
highest = lax.Precision.HIGHEST
bf16 = jnp.bfloat16
f32 = jnp.float32


def linear_table():
    points = np.array([-1.0, -1.0 / np.sqrt(5.0), 1.0 / np.sqrt(5.0), 1.0])
    return np.stack([(1.0 - points) / 2.0, (1.0 + points) / 2.0], axis=1)


def split_np(values):
    values = values.astype(np.float32)
    high = values.astype(bf16)
    low = (values - high.astype(np.float32)).astype(bf16)
    return high, low


def tables():
    linear = linear_table()
    cube = np.kron(np.kron(linear, linear), linear)
    prolong = np.kron(np.eye(NVAR), cube).astype(np.float32)
    flat = np.kron(np.eye(NVAR), np.kron(linear, linear)).astype(np.float32)
    high, low = split_np(prolong)
    lift = np.zeros((NF, 128), high.dtype)
    lift[:, :NC] = high
    lift[:, 64 : 64 + NC] = low
    wide_order = np.zeros((4, NFACE, HALO), np.float32)
    for face in range(4):
        for t in range(NCF):
            position = (t % 4) * 5 + t // 4 if face < 2 else (t % 2) * 10 + t // 2
            wide_order[face, :, position] = flat[:, t]
    face_tab = np.zeros((4, 256, 256), high.dtype)
    for face in range(4):
        high, low = split_np(wide_order[face])
        for start in (0, 128):
            face_tab[face, start : start + NFACE, :HALO] = high
            face_tab[face, start : start + NFACE, 128 : 128 + HALO] = low
    return lift, np.ascontiguousarray(prolong.T), face_tab


def halves(x):
    high = x.astype(bf16)
    low = (x - high.astype(f32)).astype(bf16)
    return high, low


def pack_left(x):
    high, low = halves(x)
    return jnp.concatenate(
        [high[:, :256], low[:, :256], jnp.concatenate([high[:, 256:], low[:, 256:]], axis=1)],
        axis=1,
    )


def pack_right(x):
    high, low = halves(x)
    both = jnp.concatenate([high, low], axis=1)
    main, rest = both[:256], both[256:]
    return jnp.concatenate([main, main, rest, rest], axis=0)


def product(left, right):
    out = jnp.dot(left, right, preferred_element_type=f32)
    return out[:, :128] + out[:, 128:]


def pad_rows(x, rows):
    return jnp.concatenate([x, jnp.zeros((rows - x.shape[0], x.shape[1]), x.dtype)], axis=0)


def pad_lanes(x, lanes):
    return jnp.concatenate([x, jnp.zeros((x.shape[0], lanes - x.shape[1]), x.dtype)], axis=1)


def twice(x, rows):
    high, low = halves(pad_rows(x, rows))
    both = jnp.concatenate([high, low], axis=1)
    return jnp.concatenate([both, both], axis=0)


def trace(ref, slot, face):
    odd = face & 1
    if face < 2:
        return jnp.concatenate(
            [ref[slot, pl.ds(64 * v + 48 * odd, 16), :] for v in range(NVAR)], axis=0
        )
    if face < 4:
        tiles = ref[slot].reshape(20, 16, RHS)[:, 8 * odd : 8 * odd + 8]
        pairs = tiles.reshape(10, 2, 8, RHS)
        first, second = pairs[:, 0], pairs[:, 1]
        upper = lax.broadcasted_iota(jnp.int32, (10, 8, RHS), 1) < 4
        if odd:
            out = jnp.where(upper, pltpu.roll(first, 4, 1), second)
        else:
            out = jnp.where(upper, first, pltpu.roll(second, 4, 1))
        return out.reshape(NFACE, RHS)
    return ref[slot, pl.ds(3 * odd, NFACE, stride=4), :]


def coarse_trace_to(ref, slot, face, out):
    odd = face & 1
    if face < 2:
        for q in range(4):
            out[pl.ds(5 * q, 5), :] = ref[slot, pl.ds(4 * odd + q, 5, stride=8), :]
    else:
        for q in range(2):
            out[pl.ds(10 * q, 10), :] = ref[slot, pl.ds(2 * odd + q, 10, stride=4), :]


def coarse_rows(face, t):
    odd = face & 1
    var = lax.shift_right_logical(t, 2)
    a = lax.shift_right_logical(t, 1) & 1
    b = t & 1
    if face < 2:
        return var * 8 + 4 * odd + a * 2 + b
    if face < 4:
        return var * 8 + a * 4 + 2 * odd + b
    return var * 8 + a * 4 + b * 2 + odd


def halo_rows(face, t):
    if face < 2:
        return (t & 3) * 5 + lax.shift_right_logical(t, 2)
    return (t & 1) * 10 + lax.shift_right_logical(t, 1)


def kernel(
    rhs_hbm, blocks_hbm, inv_hbm, lifts_hbm, coefs_hbm,
    cblocks_hbm, cinv_hbm, clifts_hbm, ccoefs_hbm, nbr, counts,
    lift_hbm, restrict_hbm, face_hbm,
    out,
    rhs, stage, inv_stage, lifts, coefs, cblocks, cinv, clifts, ccoefs, lift_tab, restrict_tab, face_tab,
    left_a, left_d, lift_h, lift_l, coef_cols, coef_sq,
    v, vpre, x_h, x_l, r_loc, cross_l, cross_g, cross_k, left_ip, coarse_m, w1, w,
    z_old, f_send, f_recv, c_send, c_recv,
    load_sem, send_sem, recv_sem,
):
    wide = lax.axis_index("wide")
    narrow = lax.axis_index("narrow")
    base = (wide * NARROW + narrow) * SLOTS
    sides = [
        (wide > 0, {"wide": wide - 1}),
        (wide < WIDE - 1, {"wide": wide + 1}),
        (narrow > 0, {"narrow": narrow - 1}),
        (narrow < NARROW - 1, {"narrow": narrow + 1}),
    ]

    loads = {}
    count = 0
    pairs = [("rhs", rhs_hbm, rhs)]
    pairs += [(("inv", e), inv_hbm.at[e], inv_stage.at[e]) for e in range(SLOTS)]
    pairs += [("lifts", lifts_hbm, lifts), ("coefs", coefs_hbm, coefs)]
    pairs += [(("blocks", e), blocks_hbm.at[e], stage.at[e]) for e in range(SLOTS)]
    pairs += [
        ("cblocks", cblocks_hbm, cblocks), ("cinv", cinv_hbm, cinv),
        ("clifts", clifts_hbm, clifts), ("ccoefs", ccoefs_hbm, ccoefs),
        ("lift", lift_hbm, lift_tab), ("restrict", restrict_hbm, restrict_tab),
        ("face", face_hbm, face_tab),
    ]
    for name, src, dst in pairs:
        loads[name] = pltpu.make_async_copy(src, dst, load_sem.at[count])
        loads[name].start()
        count += 1

    barrier = pltpu.get_barrier_semaphore()
    for has, device in sides:
        @pl.when(has)
        def _():
            pl.semaphore_signal(barrier, 1, device_id=device, device_id_type=MESH)

    for face in range(4):
        @pl.when(jnp.logical_not(sides[face][0]))
        def _():
            for r in range(3):
                f_recv[r, face] = jnp.zeros((NFACE, RHS), f32)
            for r in range(4):
                c_recv[r, face] = jnp.zeros((HALO, RHS), f32)
    for r in range(4):
        for face in range(4):
            c_send[r, face, pl.ds(16, 8), :] = jnp.zeros((8, RHS), f32)

    local, slot, cross = {}, {}, {}
    for e in range(SLOTS):
        for f in range(6):
            g = nbr[e, f]
            here = jnp.logical_and(g >= base, g < base + SLOTS)
            local[e, f] = jnp.where(here, 1, 0)
            slot[e, f] = jnp.clip(g - base, 0, SLOTS - 1)
            if f < 4:
                cross[e, f] = jnp.where(jnp.logical_and(g >= 0, jnp.logical_not(here)), 1, 0)
    owner = [
        jnp.clip(sum(e * cross[e, f] for e in range(1, SLOTS)), 0, SLOTS - 1) for f in range(4)
    ]
    weight = {key: value.astype(f32) for key, value in cross.items()}

    def transfer(send, recv, round_index, sem_row, face, target):
        return pltpu.make_async_remote_copy(
            src_ref=send.at[round_index, face],
            dst_ref=recv.at[round_index, target],
            send_sem=send_sem.at[sem_row, face],
            recv_sem=recv_sem.at[sem_row, target],
            device_id=sides[face][1],
            device_id_type=MESH,
        )

    def start_all(send, recv, round_index, sem_row):
        for face in range(4):
            @pl.when(sides[face][0])
            def _():
                transfer(send, recv, round_index, sem_row, face, face ^ 1).start()

    def wait_all(send, recv, round_index, sem_row):
        for face in range(4):
            @pl.when(sides[face][0])
            def _():
                transfer(send, recv, round_index, sem_row, face, face).wait_recv()

    def send_fine(round_index, sem_row):
        for face in range(4):
            f_send[round_index, face] = trace(v, owner[face], face)
        start_all(f_send, f_recv, round_index, sem_row)

    def send_coarse(round_index, sem_row):
        for face in range(4):
            coarse_trace_to(w, owner[face], face, c_send.at[round_index, face])
        start_all(c_send, c_recv, round_index, sem_row)

    loads["rhs"].wait()
    for e in range(SLOTS):
        live = jnp.where(e < counts[0], 1.0, 0.0)
        rhs[e] = rhs[e] * live
        loads["inv", e].wait()
        left_d[e] = pack_left(0.8 * inv_stage[e])
        v[e] = product(left_d[e], pack_right(rhs[e]))
    peers = 4 - sum(jnp.where(has, 0, 1) for has, device in sides)
    pl.semaphore_wait(barrier, peers)
    send_fine(0, 0)

    loads["lifts"].wait()
    loads["coefs"].wait()
    lift_high, lift_low = [], []
    for f in range(6):
        high, low = halves(lifts[f])
        lift_high.append(high)
        lift_low.append(low)
    gap = jnp.zeros((NF, 32), bf16)
    lift_h[...] = jnp.concatenate(lift_high + [gap], axis=1)
    lift_l[...] = jnp.concatenate(lift_low + [gap], axis=1)
    coef_sq[...] = jnp.zeros((128, 128), f32)
    for e in range(SLOTS):
        coef_sq[pl.ds(8 * e, 6), pl.ds(0, NFACE)] = coefs[e]
    columns = jnp.transpose(coef_sq[...])
    for e in range(SLOTS):
        for f in range(6):
            column = columns[:NFACE, 8 * e + f : 8 * e + f + 1] * local[e, f].astype(f32)
            coef_cols[e, f] = jnp.broadcast_to(column, (NFACE, RHS))
    x_h[pl.ds(480, 32), :] = jnp.zeros((32, SLOTS * RHS), bf16)
    x_l[pl.ds(480, 32), :] = jnp.zeros((32, SLOTS * RHS), bf16)
    for e in range(SLOTS):
        loads["blocks", e].wait()
        left_a[e] = pack_left(stage[e])

    def local_residual():
        for e in range(SLOTS):
            for f in range(6):
                high, low = halves(coef_cols[e, f] * trace(v, slot[e, f], f ^ 1))
                x_h[pl.ds(NFACE * f, NFACE), pl.ds(RHS * e, RHS)] = high
                x_l[pl.ds(NFACE * f, NFACE), pl.ds(RHS * e, RHS)] = low
        for pair in range(2):
            cols = pl.ds(256 * pair, 256)
            coupled = (
                jnp.dot(lift_h[...], x_h[:, cols], preferred_element_type=f32)
                + jnp.dot(lift_h[...], x_l[:, cols], preferred_element_type=f32)
                + jnp.dot(lift_l[...], x_h[:, cols], preferred_element_type=f32)
            )
            for half in range(2):
                e = 2 * pair + half
                block = product(left_a[e], pack_right(v[e]))
                r_loc[e] = rhs[e] - block - coupled[:, 128 * half : 128 * half + 128]

    def presweep():
        for e in range(SLOTS):
            vpre[e] = v[e] + product(left_d[e], pack_right(r_loc[e]))

    def cross_terms(left, recv, round_index):
        return [
            product(left[f], twice(recv[round_index, f], 128)) for f in range(4)
        ]

    def combine(terms, src, dst):
        for e in range(SLOTS):
            total = src[e]
            for f in range(4):
                total = total - weight[e, f] * terms[f]
            dst[e] = total

    local_residual()
    presweep()
    scaled = []
    for f in range(4):
        coef_row = coefs[owner[f], pl.ds(f, 1), :]
        scaled.append(pad_lanes(lifts[f] * coef_row, 128))
    rights = [pack_right(s) for s in scaled]
    for f in range(4):
        high, low = halves(product(left_d[owner[f]], rights[f]))
        cross_l[f] = jnp.concatenate([high, low], axis=1)

    wait_all(f_send, f_recv, 0, 0)
    combine(cross_terms(cross_l, f_recv, 0), vpre, v)
    send_fine(1, 1)

    local_residual()
    for name in ("cblocks", "cinv", "clifts", "ccoefs", "lift", "restrict", "face"):
        loads[name].wait()
    for e in range(SLOTS):
        left_ip[e] = pack_left(
            jnp.dot(0.2 * cinv[e], restrict_tab[...], precision=highest, preferred_element_type=f32)
        )
    for f in range(4):
        high, low = halves(product(left_ip[owner[f]], rights[f]))
        cross_k[f] = jnp.concatenate([high, low], axis=1)
    for e in range(SLOTS):
        w1[e] = product(left_ip[e], pack_right(r_loc[e]))
    t = lax.broadcasted_iota(jnp.int32, (128, 256), 0)
    lane = lax.broadcasted_iota(jnp.int32, (128, 256), 1)
    for e in range(SLOTS):
        def placed(matrix, target):
            high, low = halves(pad_lanes(matrix, 128))
            both = jnp.concatenate([high, low], axis=0)
            chosen = jnp.where(lane == target, 1.0, 0.0).astype(bf16)
            out = jnp.dot(both, chosen, preferred_element_type=f32)
            return out[:NC] + out[NC:]

        total = placed(cblocks[e], jnp.where(t < NC, t + NC * e, -1))
        for f in range(6):
            target = local[e, f] * (coarse_rows(f ^ 1, t) + NC * slot[e, f] + 1)
            if f < 4:
                target = target + cross[e, f] * (halo_rows(f, t) + 4 * NC + HALO * f + 1)
            target = jnp.where(t < NCF, target - 1, -1)
            total = total + placed(clifts[f] * ccoefs[e, pl.ds(f, 1), :], target)
        row = lax.broadcasted_iota(jnp.int32, (NC, 256), 0)
        col = lax.broadcasted_iota(jnp.int32, (NC, 256), 1)
        unit = jnp.where(col == row + NC * e, 1.0, 0.0)
        full = unit - jnp.dot(
            0.8 * cinv[e], total, precision=highest, preferred_element_type=f32
        )
        coarse_m[e] = full

    wait_all(f_send, f_recv, 1, 1)
    combine(cross_terms(cross_k, f_recv, 1), w1, w)
    for e in range(SLOTS):
        w1[e] = w[e]
    send_coarse(0, 2)

    left_high, left_low = halves(coarse_m[...].reshape(SLOTS * NC, 256))
    left_m = jnp.concatenate([left_high, left_low], axis=0)
    for f, term in enumerate(cross_terms(cross_l, f_recv, 1)):
        z_old[f] = term
    for f in range(4):
        high, low = halves(product(cross_l[f], face_tab[f]))
        cross_g[f] = jnp.concatenate([high, low], axis=1)

    for sweep in range(3):
        wait_all(c_send, c_recv, sweep, 2 + sweep)
        state = jnp.concatenate(
            [w[...].reshape(SLOTS * NC, RHS), c_recv[sweep].reshape(4 * HALO, RHS)], axis=0
        )
        high, low = halves(state)
        moved = jnp.dot(
            left_m, jnp.concatenate([high, low], axis=1), preferred_element_type=f32
        )
        moved = moved[: 4 * NC, :128] + (moved[: 4 * NC, 128:] + moved[4 * NC :, :128])
        w[...] = w1[...] + moved.reshape(SLOTS, NC, RHS)
        send_coarse(sweep + 1, 3 + sweep)

    for e in range(SLOTS):
        v[e] = v[e] + product(lift_tab[...], twice(w[e], 64))
    local_residual()
    presweep()
    combine([z_old[f] for f in range(4)], vpre, vpre)
    wait_all(c_send, c_recv, 3, 5)
    combine(cross_terms(cross_g, c_recv, 3), vpre, v)
    send_fine(2, 6)
    local_residual()
    presweep()
    wait_all(f_send, f_recv, 2, 6)
    combine(cross_terms(cross_l, f_recv, 2), vpre, out)

    for face in range(4):
        @pl.when(sides[face][0])
        def _():
            for r, row in ((0, 0), (1, 1), (2, 6)):
                transfer(f_send, f_recv, r, row, face, face ^ 1).wait_send()
            for r in range(4):
                transfer(c_send, c_recv, r, 2 + r, face, face ^ 1).wait_send()


def body(*args):
    any_spec = pl.BlockSpec(memory_space=pl.ANY)
    smem_spec = pl.BlockSpec(memory_space=pltpu.SMEM)
    constants = [jnp.asarray(c) for c in tables()]
    vm = pltpu.VMEM
    scratch = [
        vm((SLOTS, NF, RHS), f32), vm((SLOTS, NF, NF), f32), vm((SLOTS, NF, NF), f32),
        vm((6, NF, NFACE), f32), vm((SLOTS, 6, NFACE), f32),
        vm((SLOTS, NC, NC), f32), vm((SLOTS, NC, NC), f32), vm((6, NC, NCF), f32),
        vm((SLOTS, 6, NCF), f32),
        vm((NF, 128), bf16), vm((NC, NF), f32), vm((4, 256, 256), bf16),
        vm((SLOTS, NF, 640), bf16), vm((SLOTS, NF, 640), bf16),
        vm((NF, 512), bf16), vm((NF, 512), bf16),
        vm((SLOTS, 6, NFACE, RHS), f32), vm((128, 128), f32),
        vm((SLOTS, NF, RHS), f32), vm((SLOTS, NF, RHS), f32),
        vm((512, 512), bf16), vm((512, 512), bf16), vm((SLOTS, NF, RHS), f32),
        vm((4, NF, 256), bf16), vm((4, NF, 256), bf16), vm((4, NC, 256), bf16),
        vm((SLOTS, NC, 640), bf16), vm((SLOTS, NC, 256), f32),
        vm((SLOTS, NC, RHS), f32), vm((SLOTS, NC, RHS), f32),
        vm((4, NF, RHS), f32),
        vm((3, 4, NFACE, RHS), f32), vm((3, 4, NFACE, RHS), f32),
        vm((4, 4, HALO, RHS), f32), vm((4, 4, HALO, RHS), f32),
        pltpu.SemaphoreType.DMA((24,)),
        pltpu.SemaphoreType.DMA((7, 4)), pltpu.SemaphoreType.DMA((7, 4)),
    ]
    return pl.pallas_call(
        kernel,
        out_shape=jax.ShapeDtypeStruct((SLOTS, NF, RHS), f32),
        in_specs=[any_spec] * 9 + [smem_spec] * 2 + [any_spec] * 3,
        out_specs=pl.BlockSpec(memory_space=pltpu.VMEM),
        scratch_shapes=scratch,
        compiler_params=pltpu.CompilerParams(collective_id=0, has_side_effects=True),
        name="cycle",
    )(*args, *constants)


def solution(mesh):
    split = ("wide", "narrow")
    placed = (
        P(split, None, None),
        P(split, None, None),
        P(split, None, None),
        P(),
        P(split, None, None),
        P(split, None, None),
        P(split, None, None),
        P(),
        P(split, None, None),
        P(split, None),
        P(split),
    )
    return jax.shard_map(
        body, mesh=mesh, in_specs=placed, out_specs=P(split, None, None), check_vma=False
    )
```

time: 195 us -> 48.8 us (0.25); the launches traced: 191 us -> 48.4 us
  starting transfers between devices: 90.7 us -> 0 us
  matrix products: 49.6 us -> 0 us
  Pallas kernels: 0 us -> 39.2 us
  waiting for transfers between devices: 39.2 us -> 0 us
  other arithmetic: 2.99 us -> 0 us
  local copies, waits for them, and re-layouts: 6.34 us -> 8.63 us
    ppermute x28 -> x0, starting transfers between devices: 90.7 us -> none  [the longest x14 51.6 us: with_halo(): lax.ppermute(head, axis, [((i + 1) % count, i) for i in range(ends)])]
    dot_general x66 -> x0, matrix products: 49.6 us -> none  [the longest x42 21 us: pick_rows(): return jnp.einsum('ab,bqr->aqr', selector, candidates, precision=highest)]
    ppermute x28 -> x0, waiting for transfers between devices: 39.2 us -> none  [the longest x14 39.1 us: with_halo(): lax.ppermute(head, axis, [((i + 1) % count, i) for i in range(ends)])]
    pallas_call x0 -> x1, Pallas kernels: none -> 39.2 us  [body(): pl.pallas_call(kernel, out_shape=jax.ShapeDtypeStruct((SLOTS, NF, RHS), f...]
    unnamed x24 -> x5, local copies, waits for them, and re-layouts: 0.34 us -> 8.63 us
    slice x65 -> x0, local copies, waits for them, and re-layouts: 6 us -> none  [the longest x14 1.51 us: face_traces(): shaped[:, :, :, :, 0]]
    mul x7 -> x0, other arithmetic: 2.97 us -> none  [lift_apply(): face_coefs[:, :, :, None] * nearby]
  transfers between devices with their start and end apart: 28 -> 0, of which waited for: 7 -> 0; matrix products, arithmetic and copies ran while one was open for 9% -> 0% of each run, Pallas kernels for 0% -> 0%
where the time goes in v1:
time: 48.8 us; the launch traced here: 48.4 us
  Pallas kernels  39.2 us (80%)
  local copies, waits for them, and re-layouts  8.63 us (18%)
  between operations  0.66 us (1%)
    pallas_call x1, Pallas kernels, body(): pl.pallas_call(kernel, out_shape=jax.ShapeDtypeStruct((SLOTS, NF, RHS), f...  39.2 us
    unnamed x5, local copies, waits for them, and re-layouts  8.63 us

profile of v1, /device:TPU:103, one launch (start us, length us, event | category | flops | bytes accessed | tf_op | source)
XLA Modules:
  0.0 48.4 jit_solution(7259260327431730835)
XLA Ops:
  0.7 1.3 %copy.16.coefs_hbm = f32[4,6,80]{2,1,0:T(8,128)} copy(f32[4,6,80]{2,0,1:T(4,128)} %param.18) | data formatting | bytes 15360 | tf_op args[4]
  2.0 1.3 %copy.18.ccoefs_hbm = f32[4,6,20]{2,1,0:T(8,128)} copy(f32[4,6,20]{2,0,1:T(4,128)} %param.22) | data formatting | bytes 3840 | tf_op args[8]
  3.3 1.6 %copy.17.clifts_hbm = f32[6,40,20]{2,1,0:T(8,128)} copy(f32[6,40,20]{1,2,0:T(8,128)} %param.21) | data formatting | bytes 38400 | tf_op args[7]
  4.9 2.4 %copy.15.lifts_hbm = f32[6,320,80]{2,1,0:T(8,128)} copy(f32[6,320,80]{1,2,0:T(8,128)} %param.17) | data formatting | bytes 1228800 | tf_op args[3]
  7.3 39.2 %cycle.1 = f32[4,320,128]{2,1,0:T(8,128)} custom-call(f32[4,320,128]{2,1,0:T(8,128)} %rhs_hbm.1, f32[4,320,320]{2,1,0:T(8,128)} %blocks_hbm.1, f32[4,320,320]{2,1,0:T(8,128)} %inv_hbm.1, f32[6,320,80]{2,1,0:T(8,128)} %copy.15.lifts_hbm, f32[4,6,80]{2,1,0:T(8,128)} %copy.16.coefs_hbm, f32[4,40,40]{2,1,0:T(8,128)} %cblocks_hbm.1, f32[4,40,40]{2,1,0:T(8,128)} %cinv_hbm.1, ...), custom_call_target="tpu_custom_call" | custom-call | tf_op jit(solution)/shard_map/cycle/pallas_call | solution.py:443
  46.5 2.0 %copy.21 = f32[4,320,128]{2,1,0:T(8,128)} copy(f32[4,320,128]{2,1,0:T(8,128)} %cycle.1) | data formatting | bytes 1310720

commit v2 on v1

--- a/solution.py
+++ b/solution.py
@@ -146,14 +146,14 @@
 
 def kernel(
     rhs_hbm, blocks_hbm, inv_hbm, lifts_hbm, coefs_hbm,
-    cblocks_hbm, cinv_hbm, clifts_hbm, ccoefs_hbm, nbr, counts,
+    cblocks_hbm, cinv_hbm, clifts_hbm, ccoefs_hbm, nbr_hbm, counts,
     lift_hbm, restrict_hbm, face_hbm,
     out,
     rhs, stage, inv_stage, lifts, coefs, cblocks, cinv, clifts, ccoefs, lift_tab, restrict_tab, face_tab,
     left_a, left_d, lift_h, lift_l, coef_cols, coef_sq,
     v, vpre, x_h, x_l, r_loc, cross_l, cross_g, cross_k, left_ip, coarse_m, w1, w,
     z_old, f_send, f_recv, c_send, c_recv,
-    load_sem, send_sem, recv_sem,
+    nbr, load_sem, send_sem, recv_sem,
 ):
     wide = lax.axis_index("wide")
     narrow = lax.axis_index("narrow")
@@ -167,7 +167,7 @@
 
     loads = {}
     count = 0
-    pairs = [("rhs", rhs_hbm, rhs)]
+    pairs = [("nbr", nbr_hbm, nbr), ("rhs", rhs_hbm, rhs)]
     pairs += [(("inv", e), inv_hbm.at[e], inv_stage.at[e]) for e in range(SLOTS)]
     pairs += [("lifts", lifts_hbm, lifts), ("coefs", coefs_hbm, coefs)]
     pairs += [(("blocks", e), blocks_hbm.at[e], stage.at[e]) for e in range(SLOTS)]
@@ -199,6 +199,7 @@
         for face in range(4):
             c_send[r, face, pl.ds(16, 8), :] = jnp.zeros((8, RHS), f32)
 
+    loads["nbr"].wait()
     local, slot, cross = {}, {}, {}
     for e in range(SLOTS):
         for f in range(6):
@@ -258,21 +259,18 @@
 
     loads["lifts"].wait()
     loads["coefs"].wait()
-    lift_high, lift_low = [], []
+    flat = pad_rows(jnp.concatenate([lifts[f] for f in range(6)], axis=0), 512)
+    upright = jnp.transpose(pad_lanes(flat, 384))[:NF]
+    lift_high, lift_low = halves(upright)
+    lift_h[...] = lift_high
+    lift_l[...] = lift_low
+    coef_sq[...] = jnp.zeros((128, 128), f32)
     for f in range(6):
-        high, low = halves(lifts[f])
-        lift_high.append(high)
-        lift_low.append(low)
-    gap = jnp.zeros((NF, 32), bf16)
-    lift_h[...] = jnp.concatenate(lift_high + [gap], axis=1)
-    lift_l[...] = jnp.concatenate(lift_low + [gap], axis=1)
-    coef_sq[...] = jnp.zeros((128, 128), f32)
-    for e in range(SLOTS):
-        coef_sq[pl.ds(8 * e, 6), pl.ds(0, NFACE)] = coefs[e]
+        coef_sq[pl.ds(8 * f, SLOTS), pl.ds(0, NFACE)] = coefs[f]
     columns = jnp.transpose(coef_sq[...])
     for e in range(SLOTS):
         for f in range(6):
-            column = columns[:NFACE, 8 * e + f : 8 * e + f + 1] * local[e, f].astype(f32)
+            column = columns[:NFACE, 8 * f + e : 8 * f + e + 1] * local[e, f].astype(f32)
             coef_cols[e, f] = jnp.broadcast_to(column, (NFACE, RHS))
     x_h[pl.ds(480, 32), :] = jnp.zeros((32, SLOTS * RHS), bf16)
     x_l[pl.ds(480, 32), :] = jnp.zeros((32, SLOTS * RHS), bf16)
@@ -318,8 +316,9 @@
     presweep()
     scaled = []
     for f in range(4):
-        coef_row = coefs[owner[f], pl.ds(f, 1), :]
-        scaled.append(pad_lanes(lifts[f] * coef_row, 128))
+        coef_row = sum(weight[e, f] * coefs[f, pl.ds(e, 1), :] for e in range(SLOTS))
+        square = jnp.transpose(pad_lanes(pad_rows(lifts[f], 128), 384))[:NF]
+        scaled.append(square * pad_lanes(coef_row, 128))
     rights = [pack_right(s) for s in scaled]
     for f in range(4):
         high, low = halves(product(left_d[owner[f]], rights[f]))
@@ -341,23 +340,26 @@
         cross_k[f] = jnp.concatenate([high, low], axis=1)
     for e in range(SLOTS):
         w1[e] = product(left_ip[e], pack_right(r_loc[e]))
+    clift_sq = [
+        jnp.transpose(pad_lanes(pad_rows(clifts[f], 128), 128))[:NC] for f in range(6)
+    ]
     t = lax.broadcasted_iota(jnp.int32, (128, 256), 0)
     lane = lax.broadcasted_iota(jnp.int32, (128, 256), 1)
     for e in range(SLOTS):
         def placed(matrix, target):
-            high, low = halves(pad_lanes(matrix, 128))
+            high, low = halves(matrix)
             both = jnp.concatenate([high, low], axis=0)
             chosen = jnp.where(lane == target, 1.0, 0.0).astype(bf16)
             out = jnp.dot(both, chosen, preferred_element_type=f32)
             return out[:NC] + out[NC:]
 
-        total = placed(cblocks[e], jnp.where(t < NC, t + NC * e, -1))
+        total = placed(pad_lanes(cblocks[e], 128), jnp.where(t < NC, t + NC * e, -1))
         for f in range(6):
             target = local[e, f] * (coarse_rows(f ^ 1, t) + NC * slot[e, f] + 1)
             if f < 4:
                 target = target + cross[e, f] * (halo_rows(f, t) + 4 * NC + HALO * f + 1)
             target = jnp.where(t < NCF, target - 1, -1)
-            total = total + placed(clifts[f] * ccoefs[e, pl.ds(f, 1), :], target)
+            total = total + placed(clift_sq[f] * pad_lanes(ccoefs[f, pl.ds(e, 1), :], 128), target)
         row = lax.broadcasted_iota(jnp.int32, (NC, 256), 0)
         col = lax.broadcasted_iota(jnp.int32, (NC, 256), 1)
         unit = jnp.where(col == row + NC * e, 1.0, 0.0)
@@ -416,15 +418,22 @@
 
 
 def body(*args):
-    any_spec = pl.BlockSpec(memory_space=pl.ANY)
-    smem_spec = pl.BlockSpec(memory_space=pltpu.SMEM)
+    args = list(args)
+    for i in (3, 7):
+        args[i] = jnp.transpose(args[i], (0, 2, 1))
+    for i in (4, 8):
+        args[i] = jnp.transpose(args[i], (1, 0, 2))
+    any_spec = pl.BlockSpec(memory_space=pltpu.HBM)
     constants = [jnp.asarray(c) for c in tables()]
+    pin = lambda x: pltpu.with_memory_space_constraint(x, pltpu.HBM)
+    args = [pin(a) for a in args[:10]] + args[10:]
+    constants = [pin(c) for c in constants]
     vm = pltpu.VMEM
     scratch = [
         vm((SLOTS, NF, RHS), f32), vm((SLOTS, NF, NF), f32), vm((SLOTS, NF, NF), f32),
-        vm((6, NF, NFACE), f32), vm((SLOTS, 6, NFACE), f32),
-        vm((SLOTS, NC, NC), f32), vm((SLOTS, NC, NC), f32), vm((6, NC, NCF), f32),
-        vm((SLOTS, 6, NCF), f32),
+        vm((6, NFACE, NF), f32), vm((6, SLOTS, NFACE), f32),
+        vm((SLOTS, NC, NC), f32), vm((SLOTS, NC, NC), f32), vm((6, NCF, NC), f32),
+        vm((6, SLOTS, NCF), f32),
         vm((NF, 128), bf16), vm((NC, NF), f32), vm((4, 256, 256), bf16),
         vm((SLOTS, NF, 640), bf16), vm((SLOTS, NF, 640), bf16),
         vm((NF, 512), bf16), vm((NF, 512), bf16),
@@ -437,16 +446,17 @@
         vm((4, NF, RHS), f32),
         vm((3, 4, NFACE, RHS), f32), vm((3, 4, NFACE, RHS), f32),
         vm((4, 4, HALO, RHS), f32), vm((4, 4, HALO, RHS), f32),
+        pltpu.SMEM((SLOTS, 6), jnp.int32),
         pltpu.SemaphoreType.DMA((24,)),
         pltpu.SemaphoreType.DMA((7, 4)), pltpu.SemaphoreType.DMA((7, 4)),
     ]
     return pl.pallas_call(
         kernel,
         out_shape=jax.ShapeDtypeStruct((SLOTS, NF, RHS), f32),
-        in_specs=[any_spec] * 9 + [smem_spec] * 2 + [any_spec] * 3,
+        in_specs=[any_spec] * 10 + [pl.BlockSpec(memory_space=pltpu.SMEM)] + [any_spec] * 3,
         out_specs=pl.BlockSpec(memory_space=pltpu.VMEM),
         scratch_shapes=scratch,
-        compiler_params=pltpu.CompilerParams(collective_id=0, has_side_effects=True),
+        compiler_params=pltpu.CompilerParams(collective_id=0, has_side_effects=True, vmem_limit_bytes=32 << 20),
         name="cycle",
     )(*args, *constants)
 

time: 48.8 us -> 39.3 us (0.81)
  local copies, waits for them, and re-layouts: 8.63 us -> 0.84 us
  Pallas kernels: 39.2 us -> 37.8 us
    unnamed x5 -> x1, local copies, waits for them, and re-layouts: 8.63 us -> 0.84 us
    pallas_call x1, Pallas kernels: 39.2 us -> 37.8 us  [body(): pl.pallas_call(kernel, out_shape=jax.ShapeDtypeStruct((SLOTS, NF, RHS), f...]
where the time goes in v2:
time: 39.3 us
  Pallas kernels  37.8 us (96%)
  local copies, waits for them, and re-layouts  0.84 us (2%)
  between operations  0.66 us (2%)
    pallas_call x1, Pallas kernels, body(): pl.pallas_call(kernel, out_shape=jax.ShapeDtypeStruct((SLOTS, NF, RHS), f...  37.8 us
    unnamed x1, local copies, waits for them, and re-layouts  0.84 us

profile of v2, /device:TPU:103, one launch (start us, length us, event | category | flops | bytes accessed | tf_op | source)
XLA Modules:
  0.0 39.3 jit_solution(8072403816751075920)
XLA Ops:
  0.7 37.8 %cycle.1 = f32[4,320,128]{2,1,0:T(8,128)S(1)} custom-call(f32[4,320,128]{2,1,0:T(8,128)} %rhs_hbm.1, f32[4,320,320]{2,1,0:T(8,128)} %blocks_hbm.1, f32[4,320,320]{2,1,0:T(8,128)} %inv_hbm.1, f32[6,80,320]{2,1,0:T(8,128)} %bitcast.4, f32[6,4,80]{2,1,0:T(4,128)} %bitcast.6, f32[4,40,40]{2,1,0:T(8,128)} %cblocks_hbm.1, f32[4,40,40]{2,1,0:T(8,128)} %cinv_hbm.1, ...), custom_call_target="tpu_custom_call" | custom-call | tf_op jit(solution)/shard_map/cycle/pallas_call | solution.py:453
  38.4 0.8 %copy.17 = f32[4,320,128]{2,1,0:T(8,128)} copy(f32[4,320,128]{2,1,0:T(8,128)S(1)} %cycle.1) | data formatting | bytes 1310720

commit v3 on v2

--- a/solution.py
+++ b/solution.py
@@ -18,8 +18,14 @@
 NARROW = 32
 MESH = pl.DeviceIdType.MESH
 highest = lax.Precision.HIGHEST
+STEPS = [(-1, 0), (1, 0), (0, -1), (0, 1)]
+REACH = STEPS + [(-2, 0), (2, 0), (0, -2), (0, 2), (-1, -1), (-1, 1), (1, -1), (1, 1)]
 bf16 = jnp.bfloat16
 f32 = jnp.float32
+
+
+def offset(face, other):
+    return tuple(a + b for a, b in zip(STEPS[face], STEPS[other]))
 
 
 def linear_table():
@@ -152,22 +158,47 @@
     rhs, stage, inv_stage, lifts, coefs, cblocks, cinv, clifts, ccoefs, lift_tab, restrict_tab, face_tab,
     left_a, left_d, lift_h, lift_l, coef_cols, coef_sq,
     v, vpre, x_h, x_l, r_loc, cross_l, cross_g, cross_k, left_ip, coarse_m, w1, w,
-    z_old, f_send, f_recv, c_send, c_recv,
-    nbr, load_sem, send_sem, recv_sem,
+    z_old, f_send, f_recv, c_send, c_recv, far_recv, p_send, p_recv, o_send, o_recv, coarse_h, pre,
+    nbr, load_sem, send_sem, recv_sem, far_send_sem, far_recv_sem,
 ):
     wide = lax.axis_index("wide")
     narrow = lax.axis_index("narrow")
     base = (wide * NARROW + narrow) * SLOTS
-    sides = [
-        (wide > 0, {"wide": wide - 1}),
-        (wide < WIDE - 1, {"wide": wide + 1}),
-        (narrow > 0, {"narrow": narrow - 1}),
-        (narrow < NARROW - 1, {"narrow": narrow + 1}),
-    ]
+
+    def inside(dw, dn):
+        conditions = []
+        if dw < 0:
+            conditions.append(wide >= -dw)
+        if dw > 0:
+            conditions.append(wide < WIDE - dw)
+        if dn < 0:
+            conditions.append(narrow >= -dn)
+        if dn > 0:
+            conditions.append(narrow < NARROW - dn)
+        result = conditions[0]
+        for condition in conditions[1:]:
+            result = jnp.logical_and(result, condition)
+        return result
+
+    def place(dw, dn):
+        return (wide + dw, narrow + dn)
+
+    sides = [(inside(*STEPS[face]), place(*STEPS[face])) for face in range(4)]
+
+    barrier = pltpu.get_barrier_semaphore()
+    peers = 0
+    for dw, dn in REACH:
+        has = inside(dw, dn)
+        peers = peers + jnp.where(has, 1, 0)
+
+        @pl.when(has)
+        def _():
+            pl.semaphore_signal(barrier, 1, device_id=place(dw, dn), device_id_type=MESH)
 
     loads = {}
     count = 0
-    pairs = [("nbr", nbr_hbm, nbr), ("rhs", rhs_hbm, rhs)]
+    pairs = [("nbr", nbr_hbm, nbr)]
+    pairs += [(("rhs", e), rhs_hbm.at[e], rhs.at[e]) for e in range(SLOTS)]
     pairs += [(("inv", e), inv_hbm.at[e], inv_stage.at[e]) for e in range(SLOTS)]
     pairs += [("lifts", lifts_hbm, lifts), ("coefs", coefs_hbm, coefs)]
     pairs += [(("blocks", e), blocks_hbm.at[e], stage.at[e]) for e in range(SLOTS)]
@@ -179,25 +210,36 @@
     ]
     for name, src, dst in pairs:
         loads[name] = pltpu.make_async_copy(src, dst, load_sem.at[count])
+        count += 1
+    early = ["nbr"]
+    for e in range(SLOTS):
+        early += [("rhs", e), ("inv", e)]
+    late = [name for name in loads if name not in early]
+    for name in early:
         loads[name].start()
-        count += 1
-
-    barrier = pltpu.get_barrier_semaphore()
-    for has, device in sides:
-        @pl.when(has)
-        def _():
-            pl.semaphore_signal(barrier, 1, device_id=device, device_id_type=MESH)
 
     for face in range(4):
         @pl.when(jnp.logical_not(sides[face][0]))
         def _():
             for r in range(3):
                 f_recv[r, face] = jnp.zeros((NFACE, RHS), f32)
-            for r in range(4):
+            for r in range(2):
                 c_recv[r, face] = jnp.zeros((HALO, RHS), f32)
-    for r in range(4):
-        for face in range(4):
-            c_send[r, face, pl.ds(16, 8), :] = jnp.zeros((8, RHS), f32)
+                p_recv[r, face] = jnp.zeros((HALO, RHS), f32)
+            o_recv[face] = jnp.zeros((HALO, RHS), f32)
+    tail = jnp.zeros((8, RHS), f32)
+    for face in range(4):
+        for r in range(2):
+            c_send[r, face, pl.ds(16, 8), :] = tail
+            p_send[r, face, pl.ds(16, 8), :] = tail
+            far_recv[r, face, pl.ds(4 * HALO, 32), :] = jnp.zeros((32, RHS), f32)
+        o_send[face, pl.ds(16, 8), :] = tail
+        for other in range(4):
+            if other != face ^ 1:
+                @pl.when(jnp.logical_not(inside(*offset(face, other))))
+                def _():
+                    for r in range(2):
+                        far_recv[r, face, pl.ds(HALO * other, HALO), :] = jnp.zeros((HALO, RHS), f32)
 
     loads["nbr"].wait()
     local, slot, cross = {}, {}, {}
@@ -236,24 +278,74 @@
             def _():
                 transfer(send, recv, round_index, sem_row, face, face).wait_recv()
 
+    def op_copy(face, target):
+        return pltpu.make_async_remote_copy(
+            src_ref=o_send.at[face],
+            dst_ref=o_recv.at[target],
+            send_sem=send_sem.at[7, face],
+            recv_sem=recv_sem.at[7, target],
+            device_id=sides[face][1],
+            device_id_type=MESH,
+        )
+
     def send_fine(round_index, sem_row):
         for face in range(4):
             f_send[round_index, face] = trace(v, owner[face], face)
         start_all(f_send, f_recv, round_index, sem_row)
 
+    def far_copy(round_index, face, other, device):
+        return pltpu.make_async_remote_copy(
+            src_ref=c_send.at[round_index, face],
+            dst_ref=far_recv.at[round_index, other ^ 1, pl.ds(HALO * (face ^ 1), HALO)],
+            send_sem=far_send_sem.at[round_index, face, other],
+            recv_sem=far_recv_sem.at[round_index, other ^ 1, face ^ 1],
+            device_id=device,
+            device_id_type=MESH,
+        )
+
+    def far_each(act):
+        for face in range(4):
+            for other in range(4):
+                if other != face ^ 1:
+                    @pl.when(inside(*offset(face, other)))
+                    def _():
+                        act(face, other, place(*offset(face, other)))
+
+    def far_start(round_index):
+        far_each(lambda face, other, device: far_copy(round_index, face, other, device).start())
+
+    def far_wait(round_index):
+        far_each(
+            lambda face, other, device: far_copy(
+                round_index, other ^ 1, face ^ 1, device
+            ).wait_recv()
+        )
+
     def send_coarse(round_index, sem_row):
         for face in range(4):
             coarse_trace_to(w, owner[face], face, c_send.at[round_index, face])
         start_all(c_send, c_recv, round_index, sem_row)
-
-    loads["rhs"].wait()
-    for e in range(SLOTS):
+        far_start(round_index)
+        for face in range(4):
+            far_recv[round_index, face, pl.ds(HALO * (face ^ 1), HALO), :] = c_send[
+                round_index, face
+            ]
+
+    def send_ahead(round_index, sem_row):
+        for face in range(4):
+            coarse_trace_to(pre, owner[face], face, p_send.at[round_index, face])
+        start_all(p_send, p_recv, round_index, sem_row)
+
+    for e in range(SLOTS):
+        loads["rhs", e].wait()
         live = jnp.where(e < counts[0], 1.0, 0.0)
         rhs[e] = rhs[e] * live
         loads["inv", e].wait()
+        if e == 2:
+            for name in late:
+                loads[name].start()
         left_d[e] = pack_left(0.8 * inv_stage[e])
         v[e] = product(left_d[e], pack_right(rhs[e]))
-    peers = 4 - sum(jnp.where(has, 0, 1) for has, device in sides)
     pl.semaphore_wait(barrier, peers)
     send_fine(0, 0)
 
@@ -300,10 +392,8 @@
         for e in range(SLOTS):
             vpre[e] = v[e] + product(left_d[e], pack_right(r_loc[e]))
 
-    def cross_terms(left, recv, round_index):
-        return [
-            product(left[f], twice(recv[round_index, f], 128)) for f in range(4)
-        ]
+    def cross_terms(left, recv):
+        return [product(left[f], twice(recv[f], 128)) for f in range(4)]
 
     def combine(terms, src, dst):
         for e in range(SLOTS):
@@ -325,7 +415,7 @@
         cross_l[f] = jnp.concatenate([high, low], axis=1)
 
     wait_all(f_send, f_recv, 0, 0)
-    combine(cross_terms(cross_l, f_recv, 0), vpre, v)
+    combine(cross_terms(cross_l, f_recv.at[0]), vpre, v)
     send_fine(1, 1)
 
     local_residual()
@@ -353,68 +443,115 @@
             out = jnp.dot(both, chosen, preferred_element_type=f32)
             return out[:NC] + out[NC:]
 
-        total = placed(pad_lanes(cblocks[e], 128), jnp.where(t < NC, t + NC * e, -1))
+        total = placed(pad_lanes(cblocks[e], 128), jnp.where(t < NC, t + 4 * HALO + NC * e, -1))
         for f in range(6):
-            target = local[e, f] * (coarse_rows(f ^ 1, t) + NC * slot[e, f] + 1)
+            target = local[e, f] * (coarse_rows(f ^ 1, t) + 4 * HALO + NC * slot[e, f] + 1)
             if f < 4:
-                target = target + cross[e, f] * (halo_rows(f, t) + 4 * NC + HALO * f + 1)
+                target = target + cross[e, f] * (halo_rows(f, t) + HALO * f + 1)
             target = jnp.where(t < NCF, target - 1, -1)
             total = total + placed(clift_sq[f] * pad_lanes(ccoefs[f, pl.ds(e, 1), :], 128), target)
         row = lax.broadcasted_iota(jnp.int32, (NC, 256), 0)
         col = lax.broadcasted_iota(jnp.int32, (NC, 256), 1)
-        unit = jnp.where(col == row + NC * e, 1.0, 0.0)
+        unit = jnp.where(col == row + 4 * HALO + NC * e, 1.0, 0.0)
         full = unit - jnp.dot(
             0.8 * cinv[e], total, precision=highest, preferred_element_type=f32
         )
         coarse_m[e] = full
+        coarse_h[e] = full[:, :128]
+    for face in range(4):
+        coarse_trace_to(coarse_h, owner[face], face, o_send.at[face])
+        @pl.when(sides[face][0])
+        def _():
+            op_copy(face, face ^ 1).start()
 
     wait_all(f_send, f_recv, 1, 1)
-    combine(cross_terms(cross_k, f_recv, 1), w1, w)
+    combine(cross_terms(cross_k, f_recv.at[1]), w1, w)
     for e in range(SLOTS):
         w1[e] = w[e]
     send_coarse(0, 2)
 
     left_high, left_low = halves(coarse_m[...].reshape(SLOTS * NC, 256))
     left_m = jnp.concatenate([left_high, left_low], axis=0)
-    for f, term in enumerate(cross_terms(cross_l, f_recv, 1)):
+
+    def quarters(left, right):
+        high, low = halves(right)
+        moved = jnp.dot(left, jnp.concatenate([high, low], axis=1), preferred_element_type=f32)
+        rows = left.shape[0] // 2
+        return moved[:rows, :128] + (moved[:rows, 128:] + moved[rows:, :128])
+
+    def local_ahead(sem_row, round_index):
+        state = jnp.concatenate(
+            [jnp.zeros((4 * HALO, RHS), f32), w[...].reshape(SLOTS * NC, RHS)], axis=0
+        )
+        pre[...] = w1[...] + quarters(left_m, state).reshape(SLOTS, NC, RHS)
+        send_ahead(round_index, sem_row)
+
+    local_ahead(4, 0)
+    for f, term in enumerate(cross_terms(cross_l, f_recv.at[1])):
         z_old[f] = term
     for f in range(4):
         high, low = halves(product(cross_l[f], face_tab[f]))
         cross_g[f] = jnp.concatenate([high, low], axis=1)
-
-    for sweep in range(3):
-        wait_all(c_send, c_recv, sweep, 2 + sweep)
-        state = jnp.concatenate(
-            [w[...].reshape(SLOTS * NC, RHS), c_recv[sweep].reshape(4 * HALO, RHS)], axis=0
-        )
-        high, low = halves(state)
-        moved = jnp.dot(
-            left_m, jnp.concatenate([high, low], axis=1), preferred_element_type=f32
-        )
-        moved = moved[: 4 * NC, :128] + (moved[: 4 * NC, 128:] + moved[4 * NC :, :128])
-        w[...] = w1[...] + moved.reshape(SLOTS, NC, RHS)
-        send_coarse(sweep + 1, 3 + sweep)
+    for face in range(4):
+        @pl.when(sides[face][0])
+        def _():
+            op_copy(face, face).wait_recv()
+    blank = jnp.zeros((HALO, 128), f32)
+    keep = lax.broadcasted_iota(jnp.int32, (HALO, 128), 1) < 4 * HALO
+    op_rows = []
+    for face in range(4):
+        block = jnp.where(keep, o_recv[face], 0.0)
+        op_rows.append(
+            jnp.concatenate([block if k == face else blank for k in range(4)], axis=1)
+        )
+    op_high, op_low = halves(jnp.concatenate(op_rows, axis=0))
+    op_left = jnp.concatenate([op_high, op_low], axis=0)
+
+    def two_steps(round_index, near_row, ahead_row):
+        wait_all(c_send, c_recv, round_index, near_row)
+        first = quarters(
+            left_m[:, :128], pad_rows(c_recv[round_index].reshape(4 * HALO, RHS), 128)
+        )
+        middle = pre[...].reshape(SLOTS * NC, RHS) + first
+        wait_all(p_send, p_recv, round_index, ahead_row)
+        far_wait(round_index)
+        halo = p_recv[round_index].reshape(4 * HALO, RHS) + quarters(
+            op_left, far_recv[round_index].reshape(512, RHS)
+        )
+        return middle, halo
+
+    middle, halo = two_steps(0, 2, 4)
+    ahead = quarters(left_m, jnp.concatenate([halo, middle], axis=0))
+    w[...] = w1[...] + ahead.reshape(SLOTS, NC, RHS)
+    send_coarse(1, 3)
+    local_ahead(5, 1)
+    middle, halo = two_steps(1, 3, 5)
+    w[...] = middle.reshape(SLOTS, NC, RHS)
 
     for e in range(SLOTS):
         v[e] = v[e] + product(lift_tab[...], twice(w[e], 64))
     local_residual()
     presweep()
     combine([z_old[f] for f in range(4)], vpre, vpre)
-    wait_all(c_send, c_recv, 3, 5)
-    combine(cross_terms(cross_g, c_recv, 3), vpre, v)
+    last = [halo[HALO * f : HALO * f + HALO] for f in range(4)]
+    combine(cross_terms(cross_g, last), vpre, v)
     send_fine(2, 6)
     local_residual()
     presweep()
     wait_all(f_send, f_recv, 2, 6)
-    combine(cross_terms(cross_l, f_recv, 2), vpre, out)
+    combine(cross_terms(cross_l, f_recv.at[2]), vpre, out)
 
     for face in range(4):
         @pl.when(sides[face][0])
         def _():
             for r, row in ((0, 0), (1, 1), (2, 6)):
                 transfer(f_send, f_recv, r, row, face, face ^ 1).wait_send()
-            for r in range(4):
+            for r in range(2):
                 transfer(c_send, c_recv, r, 2 + r, face, face ^ 1).wait_send()
+                transfer(p_send, p_recv, r, 4 + r, face, face ^ 1).wait_send()
+            op_copy(face, face ^ 1).wait_send()
+    for r in range(2):
+        far_each(lambda face, other, device: far_copy(r, face, other, device).wait_send())
 
 
 def body(*args):
@@ -445,10 +582,15 @@
         vm((SLOTS, NC, RHS), f32), vm((SLOTS, NC, RHS), f32),
         vm((4, NF, RHS), f32),
         vm((3, 4, NFACE, RHS), f32), vm((3, 4, NFACE, RHS), f32),
-        vm((4, 4, HALO, RHS), f32), vm((4, 4, HALO, RHS), f32),
+        vm((2, 4, HALO, RHS), f32), vm((2, 4, HALO, RHS), f32),
+        vm((2, 4, 128, RHS), f32),
+        vm((2, 4, HALO, RHS), f32), vm((2, 4, HALO, RHS), f32),
+        vm((4, HALO, RHS), f32), vm((4, HALO, RHS), f32),
+        vm((SLOTS, NC, 128), f32), vm((SLOTS, NC, RHS), f32),
         pltpu.SMEM((SLOTS, 6), jnp.int32),
         pltpu.SemaphoreType.DMA((24,)),
-        pltpu.SemaphoreType.DMA((7, 4)), pltpu.SemaphoreType.DMA((7, 4)),
+        pltpu.SemaphoreType.DMA((8, 4)), pltpu.SemaphoreType.DMA((8, 4)),
+        pltpu.SemaphoreType.DMA((2, 4, 4)), pltpu.SemaphoreType.DMA((2, 4, 4)),
     ]
     return pl.pallas_call(
         kernel,

time: 39.3 us -> 38 us (0.967)
  Pallas kernels: 37.8 us -> 36.4 us
    pallas_call x1, Pallas kernels: 37.8 us -> 36.4 us  [body(): pl.pallas_call(kernel, out_shape=jax.ShapeDtypeStruct((SLOTS, NF, RHS), f...]
where the time goes in v3:
time: 38 us; the launch traced here: 37.9 us
  Pallas kernels  36.4 us (96%)
  local copies, waits for them, and re-layouts  0.84 us (2%)
  between operations  0.66 us (2%)
    pallas_call x1, Pallas kernels, body(): pl.pallas_call(kernel, out_shape=jax.ShapeDtypeStruct((SLOTS, NF, RHS), f...  36.4 us
    unnamed x1, local copies, waits for them, and re-layouts  0.84 us

profile of v3, /device:TPU:103, one launch (start us, length us, event | category | flops | bytes accessed | tf_op | source)
XLA Modules:
  0.0 37.9 jit_solution(6145403386769088835)
XLA Ops:
  0.7 36.4 %cycle.1 = f32[4,320,128]{2,1,0:T(8,128)S(1)} custom-call(f32[4,320,128]{2,1,0:T(8,128)} %rhs_hbm.1, f32[4,320,320]{2,1,0:T(8,128)} %blocks_hbm.1, f32[4,320,320]{2,1,0:T(8,128)} %inv_hbm.1, f32[6,80,320]{2,1,0:T(8,128)} %bitcast.4, f32[6,4,80]{2,1,0:T(4,128)} %bitcast.6, f32[4,40,40]{2,1,0:T(8,128)} %cblocks_hbm.1, f32[4,40,40]{2,1,0:T(8,128)} %cinv_hbm.1, ...), custom_call_target="tpu_custom_call" | custom-call | tf_op jit(solution)/shard_map/cycle/pallas_call | solution.py:595
  37.1 0.8 %copy.17 = f32[4,320,128]{2,1,0:T(8,128)} copy(f32[4,320,128]{2,1,0:T(8,128)S(1)} %cycle.1) | data formatting | bytes 1310720

commit v4 on v3

--- a/solution.py
+++ b/solution.py
@@ -49,17 +49,10 @@
     lift = np.zeros((NF, 128), high.dtype)
     lift[:, :NC] = high
     lift[:, 64 : 64 + NC] = low
-    wide_order = np.zeros((4, NFACE, HALO), np.float32)
-    for face in range(4):
-        for t in range(NCF):
-            position = (t % 4) * 5 + t // 4 if face < 2 else (t % 2) * 10 + t // 2
-            wide_order[face, :, position] = flat[:, t]
-    face_tab = np.zeros((4, 256, 256), high.dtype)
-    for face in range(4):
-        high, low = split_np(wide_order[face])
-        for start in (0, 128):
-            face_tab[face, start : start + NFACE, :HALO] = high
-            face_tab[face, start : start + NFACE, 128 : 128 + HALO] = low
+    high, low = split_np(flat)
+    face_tab = np.zeros((2 * NFACE, 128), high.dtype)
+    face_tab[:NFACE, :NCF] = high
+    face_tab[NFACE:, :NCF] = low
     return lift, np.ascontiguousarray(prolong.T), face_tab
 
 
@@ -110,15 +103,16 @@
             [ref[slot, pl.ds(64 * v + 48 * odd, 16), :] for v in range(NVAR)], axis=0
         )
     if face < 4:
-        tiles = ref[slot].reshape(20, 16, RHS)[:, 8 * odd : 8 * odd + 8]
-        pairs = tiles.reshape(10, 2, 8, RHS)
+        lanes = ref.shape[-1]
+        tiles = ref[slot].reshape(20, 16, lanes)[:, 8 * odd : 8 * odd + 8]
+        pairs = tiles.reshape(10, 2, 8, lanes)
         first, second = pairs[:, 0], pairs[:, 1]
-        upper = lax.broadcasted_iota(jnp.int32, (10, 8, RHS), 1) < 4
+        upper = lax.broadcasted_iota(jnp.int32, (10, 8, lanes), 1) < 4
         if odd:
             out = jnp.where(upper, pltpu.roll(first, 4, 1), second)
         else:
             out = jnp.where(upper, first, pltpu.roll(second, 4, 1))
-        return out.reshape(NFACE, RHS)
+        return out.reshape(NFACE, lanes)
     return ref[slot, pl.ds(3 * odd, NFACE, stride=4), :]
 
 
@@ -157,8 +151,8 @@
     out,
     rhs, stage, inv_stage, lifts, coefs, cblocks, cinv, clifts, ccoefs, lift_tab, restrict_tab, face_tab,
     left_a, left_d, lift_h, lift_l, coef_cols, coef_sq,
-    v, vpre, x_h, x_l, r_loc, cross_l, cross_g, cross_k, left_ip, coarse_m, w1, w,
-    z_old, f_send, f_recv, c_send, c_recv, far_recv, p_send, p_recv, o_send, o_recv, coarse_h, pre,
+    v, vpre, x_h, x_l, r_loc, cross_l, left_r, full_r, coef_raw, cross_k, left_ip, coarse_m, w1, w,
+    f_send, f_recv, c_send, c_recv, far_recv, p_send, p_recv, o_send, o_recv, coarse_h, pre,
     nbr, load_sem, send_sem, recv_sem, far_send_sem, far_recv_sem,
 ):
     wide = lax.axis_index("wide")
@@ -215,7 +209,8 @@
     for e in range(SLOTS):
         early += [("rhs", e), ("inv", e)]
     late = [name for name in loads if name not in early]
-    for name in early:
+    first = early
+    for name in first:
         loads[name].start()
 
     for face in range(4):
@@ -241,6 +236,9 @@
                     for r in range(2):
                         far_recv[r, face, pl.ds(HALO * other, HALO), :] = jnp.zeros((HALO, RHS), f32)
 
+    for name in early:
+        if name not in first:
+            loads[name].start()
     loads["nbr"].wait()
     local, slot, cross = {}, {}, {}
     for e in range(SLOTS):
@@ -304,12 +302,11 @@
         )
 
     def far_each(act):
-        for face in range(4):
-            for other in range(4):
-                if other != face ^ 1:
-                    @pl.when(inside(*offset(face, other)))
-                    def _():
-                        act(face, other, place(*offset(face, other)))
+        turns = [(a, b) for a in range(4) for b in range(4) if a // 2 != b // 2]
+        for face, other in turns + [(a, a) for a in range(4)]:
+            @pl.when(inside(*offset(face, other)))
+            def _():
+                act(face, other, place(*offset(face, other)))
 
     def far_start(round_index):
         far_each(lambda face, other, device: far_copy(round_index, face, other, device).start())
@@ -324,8 +321,8 @@
     def send_coarse(round_index, sem_row):
         for face in range(4):
             coarse_trace_to(w, owner[face], face, c_send.at[round_index, face])
+        far_start(round_index)
         start_all(c_send, c_recv, round_index, sem_row)
-        far_start(round_index)
         for face in range(4):
             far_recv[round_index, face, pl.ds(HALO * (face ^ 1), HALO), :] = c_send[
                 round_index, face
@@ -362,8 +359,10 @@
     columns = jnp.transpose(coef_sq[...])
     for e in range(SLOTS):
         for f in range(6):
-            column = columns[:NFACE, 8 * f + e : 8 * f + e + 1] * local[e, f].astype(f32)
-            coef_cols[e, f] = jnp.broadcast_to(column, (NFACE, RHS))
+            column = columns[:NFACE, 8 * f + e : 8 * f + e + 1]
+            column = jnp.broadcast_to(column, (NFACE, RHS))
+            coef_raw[e, f] = column
+            coef_cols[e, f] = column * local[e, f].astype(f32)
     x_h[pl.ds(480, 32), :] = jnp.zeros((32, SLOTS * RHS), bf16)
     x_l[pl.ds(480, 32), :] = jnp.zeros((32, SLOTS * RHS), bf16)
     for e in range(SLOTS):
@@ -388,8 +387,8 @@
                 block = product(left_a[e], pack_right(v[e]))
                 r_loc[e] = rhs[e] - block - coupled[:, 128 * half : 128 * half + 128]
 
-    def presweep():
-        for e in range(SLOTS):
+    def presweep(which=range(SLOTS)):
+        for e in which:
             vpre[e] = v[e] + product(left_d[e], pack_right(r_loc[e]))
 
     def cross_terms(left, recv):
@@ -433,23 +432,36 @@
     clift_sq = [
         jnp.transpose(pad_lanes(pad_rows(clifts[f], 128), 128))[:NC] for f in range(6)
     ]
-    t = lax.broadcasted_iota(jnp.int32, (128, 256), 0)
-    lane = lax.broadcasted_iota(jnp.int32, (128, 256), 1)
-    for e in range(SLOTS):
-        def placed(matrix, target):
-            high, low = halves(matrix)
-            both = jnp.concatenate([high, low], axis=0)
-            chosen = jnp.where(lane == target, 1.0, 0.0).astype(bf16)
-            out = jnp.dot(both, chosen, preferred_element_type=f32)
-            return out[:NC] + out[NC:]
-
-        total = placed(pad_lanes(cblocks[e], 128), jnp.where(t < NC, t + 4 * HALO + NC * e, -1))
-        for f in range(6):
+
+    def one_hot(rows, make):
+        t = lax.broadcasted_iota(jnp.int32, (rows, 256), 0)
+        lane = lax.broadcasted_iota(jnp.int32, (rows, 256), 1)
+        return jnp.where(lane == make(t), 1.0, 0.0).astype(bf16)
+
+    def face_target(e, f):
+        def make(t):
             target = local[e, f] * (coarse_rows(f ^ 1, t) + 4 * HALO + NC * slot[e, f] + 1)
             if f < 4:
                 target = target + cross[e, f] * (halo_rows(f, t) + HALO * f + 1)
-            target = jnp.where(t < NCF, target - 1, -1)
-            total = total + placed(clift_sq[f] * pad_lanes(ccoefs[f, pl.ds(e, 1), :], 128), target)
+            return jnp.where(t < NCF, target - 1, -1)
+
+        return one_hot(32, make)
+
+    def placed(matrix, chosen):
+        high, low = halves(matrix)
+        out = jnp.dot(
+            jnp.concatenate([high, low], axis=0), chosen, preferred_element_type=f32
+        )
+        return out[:NC] + out[NC:]
+
+    for e in range(SLOTS):
+        start = 4 * HALO + NC * e
+        total = placed(
+            pad_lanes(cblocks[e], 128), one_hot(128, lambda t: jnp.where(t < NC, t + start, -1))
+        )
+        for f in range(6):
+            scaled_lift = clift_sq[f] * pad_lanes(ccoefs[f, pl.ds(e, 1), :], 128)
+            total = total + placed(scaled_lift[:, :32], face_target(e, f))
         row = lax.broadcasted_iota(jnp.int32, (NC, 256), 0)
         col = lax.broadcasted_iota(jnp.int32, (NC, 256), 1)
         unit = jnp.where(col == row + 4 * HALO + NC * e, 1.0, 0.0)
@@ -487,11 +499,6 @@
         send_ahead(round_index, sem_row)
 
     local_ahead(4, 0)
-    for f, term in enumerate(cross_terms(cross_l, f_recv.at[1])):
-        z_old[f] = term
-    for f in range(4):
-        high, low = halves(product(cross_l[f], face_tab[f]))
-        cross_g[f] = jnp.concatenate([high, low], axis=1)
     for face in range(4):
         @pl.when(sides[face][0])
         def _():
@@ -504,38 +511,98 @@
         op_rows.append(
             jnp.concatenate([block if k == face else blank for k in range(4)], axis=1)
         )
-    op_high, op_low = halves(jnp.concatenate(op_rows, axis=0))
+    op_full = jnp.concatenate(op_rows, axis=0)
+    op_high, op_low = halves(op_full)
     op_left = jnp.concatenate([op_high, op_low], axis=0)
 
-    def two_steps(round_index, near_row, ahead_row):
+    def wide_product(left, right):
+        high, low = halves(right)
+        both = jnp.concatenate([high, low], axis=1)
+        main, rest = both[:256], both[256:]
+        out = jnp.dot(
+            left,
+            jnp.concatenate([main, main, rest, rest], axis=0),
+            preferred_element_type=f32,
+        )
+        return out[:, :256] + out[:, 256:]
+
+    def correction(pair):
+        for half in range(2):
+            e = 2 * pair + half
+            for f in range(6):
+                out = jnp.dot(
+                    face_tab[:, :32], face_target(e, f), preferred_element_type=f32
+                )
+                coef = coef_raw[e, f]
+                high, low = halves(
+                    (out[:NFACE] + out[NFACE:]) * jnp.concatenate([coef, coef], axis=1)
+                )
+                x_h[pl.ds(NFACE * f, NFACE), pl.ds(256 * half, 256)] = high
+                x_l[pl.ds(NFACE * f, NFACE), pl.ds(256 * half, 256)] = low
+        for half in range(2):
+            e = 2 * pair + half
+            cols = pl.ds(256 * half, 256)
+            start = 4 * HALO + NC * e
+            coupled = (
+                jnp.dot(lift_h[...], x_h[:, cols], preferred_element_type=f32)
+                + jnp.dot(lift_h[...], x_l[:, cols], preferred_element_type=f32)
+                + jnp.dot(lift_l[...], x_h[:, cols], preferred_element_type=f32)
+            )
+            chosen = one_hot(
+                128, lambda t: jnp.where((t & 63) < NC, (t & 63) + start, -1)
+            )
+            prolonged = jnp.dot(lift_tab[...], chosen, preferred_element_type=f32)
+            coupled = coupled + wide_product(left_a[e], prolonged)
+            full = prolonged - wide_product(left_d[e], coupled)
+            full_r[e] = full
+            high, low = halves(full)
+            left_r[e] = jnp.concatenate([high, low], axis=0)
+
+    correction(0)
+    presweep(range(2))
+
+    def one_step(round_index, near_row, ahead_row):
         wait_all(c_send, c_recv, round_index, near_row)
         first = quarters(
             left_m[:, :128], pad_rows(c_recv[round_index].reshape(4 * HALO, RHS), 128)
         )
         middle = pre[...].reshape(SLOTS * NC, RHS) + first
         wait_all(p_send, p_recv, round_index, ahead_row)
-        far_wait(round_index)
-        halo = p_recv[round_index].reshape(4 * HALO, RHS) + quarters(
-            op_left, far_recv[round_index].reshape(512, RHS)
-        )
-        return middle, halo
-
-    middle, halo = two_steps(0, 2, 4)
-    ahead = quarters(left_m, jnp.concatenate([halo, middle], axis=0))
+        return jnp.concatenate([p_recv[round_index].reshape(4 * HALO, RHS), middle], axis=0)
+
+    state = one_step(0, 2, 4)
+    far_wait(0)
+    halo = state[: 4 * HALO] + quarters(op_left, far_recv[0].reshape(512, RHS))
+    ahead = quarters(left_m, jnp.concatenate([halo, state[4 * HALO :]], axis=0))
     w[...] = w1[...] + ahead.reshape(SLOTS, NC, RHS)
     send_coarse(1, 3)
     local_ahead(5, 1)
-    middle, halo = two_steps(1, 3, 5)
-    w[...] = middle.reshape(SLOTS, NC, RHS)
-
-    for e in range(SLOTS):
-        v[e] = v[e] + product(lift_tab[...], twice(w[e], 64))
-    local_residual()
-    presweep()
-    combine([z_old[f] for f in range(4)], vpre, vpre)
-    last = [halo[HALO * f : HALO * f + HALO] for f in range(4)]
-    combine(cross_terms(cross_g, last), vpre, v)
-    send_fine(2, 6)
+    correction(1)
+    presweep(range(2, SLOTS))
+    combine(cross_terms(cross_l, f_recv.at[1]), vpre, vpre)
+    lines = [trace(full_r, owner[face], face) for face in range(4)]
+    high, low = halves(jnp.concatenate(lines, axis=0))
+    left_t = jnp.concatenate([high, low], axis=0)
+    for face in range(4):
+        f_send[2, face] = trace(vpre, owner[face], face)
+
+    state = one_step(1, 3, 5)
+    far_wait(1)
+    halo = state[: 4 * HALO] + quarters(op_left, far_recv[1].reshape(512, RHS))
+    high, low = halves(jnp.concatenate([halo, state[4 * HALO :]], axis=0))
+    state = jnp.concatenate([high, low], axis=1)
+
+    def moved_by(left):
+        rows = left.shape[0] // 2
+        moved = jnp.dot(left, state, preferred_element_type=f32)
+        return moved[:rows, :128] + (moved[:rows, 128:] + moved[rows:, :128])
+
+    moved = moved_by(left_t)
+    for face in range(4):
+        f_send[2, face] = f_send[2, face] + moved[NFACE * face : NFACE * face + NFACE]
+    start_all(f_send, f_recv, 2, 6)
+    for e in range(SLOTS):
+        v[e] = vpre[e] + moved_by(left_r[e])
     local_residual()
     presweep()
     wait_all(f_send, f_recv, 2, 6)
@@ -571,16 +638,15 @@
         vm((6, NFACE, NF), f32), vm((6, SLOTS, NFACE), f32),
         vm((SLOTS, NC, NC), f32), vm((SLOTS, NC, NC), f32), vm((6, NCF, NC), f32),
         vm((6, SLOTS, NCF), f32),
-        vm((NF, 128), bf16), vm((NC, NF), f32), vm((4, 256, 256), bf16),
+        vm((NF, 128), bf16), vm((NC, NF), f32), vm((2 * NFACE, 128), bf16),
         vm((SLOTS, NF, 640), bf16), vm((SLOTS, NF, 640), bf16),
         vm((NF, 512), bf16), vm((NF, 512), bf16),
         vm((SLOTS, 6, NFACE, RHS), f32), vm((128, 128), f32),
         vm((SLOTS, NF, RHS), f32), vm((SLOTS, NF, RHS), f32),
         vm((512, 512), bf16), vm((512, 512), bf16), vm((SLOTS, NF, RHS), f32),
-        vm((4, NF, 256), bf16), vm((4, NF, 256), bf16), vm((4, NC, 256), bf16),
+        vm((4, NF, 256), bf16), vm((SLOTS, 2 * NF, 256), bf16), vm((SLOTS, NF, 256), f32), vm((SLOTS, 6, NFACE, RHS), f32), vm((4, NC, 256), bf16),
         vm((SLOTS, NC, 640), bf16), vm((SLOTS, NC, 256), f32),
         vm((SLOTS, NC, RHS), f32), vm((SLOTS, NC, RHS), f32),
-        vm((4, NF, RHS), f32),
         vm((3, 4, NFACE, RHS), f32), vm((3, 4, NFACE, RHS), f32),
         vm((2, 4, HALO, RHS), f32), vm((2, 4, HALO, RHS), f32),
         vm((2, 4, 128, RHS), f32),

time: 38 us -> 37 us (0.974)
  Pallas kernels: 36.4 us -> 35.4 us
    pallas_call x1, Pallas kernels: 36.4 us -> 35.4 us  [body(): pl.pallas_call(kernel, out_shape=jax.ShapeDtypeStruct((SLOTS, NF, RHS), f...]
where the time goes in v4:
time: 37 us; the launch traced here: 36.9 us
  Pallas kernels  35.4 us (96%)
  local copies, waits for them, and re-layouts  0.84 us (2%)
  between operations  0.66 us (2%)
    pallas_call x1, Pallas kernels, body(): pl.pallas_call(kernel, out_shape=jax.ShapeDtypeStruct((SLOTS, NF, RHS), f...  35.4 us
    unnamed x1, local copies, waits for them, and re-layouts  0.84 us

profile of v4, /device:TPU:103, one launch (start us, length us, event | category | flops | bytes accessed | tf_op | source)
XLA Modules:
  0.0 36.9 jit_solution(389880177400278037)
XLA Ops:
  0.7 35.4 %cycle.1 = f32[4,320,128]{2,1,0:T(8,128)S(1)} custom-call(f32[4,320,128]{2,1,0:T(8,128)} %rhs_hbm.1, f32[4,320,320]{2,1,0:T(8,128)} %blocks_hbm.1, f32[4,320,320]{2,1,0:T(8,128)} %inv_hbm.1, f32[6,80,320]{2,1,0:T(8,128)} %bitcast.4, f32[6,4,80]{2,1,0:T(4,128)} %bitcast.6, f32[4,40,40]{2,1,0:T(8,128)} %cblocks_hbm.1, f32[4,40,40]{2,1,0:T(8,128)} %cinv_hbm.1, ...), custom_call_target="tpu_custom_call" | custom-call | tf_op jit(solution)/shard_map/cycle/pallas_call | solution.py:661
  36.0 0.8 %copy.17 = f32[4,320,128]{2,1,0:T(8,128)} copy(f32[4,320,128]{2,1,0:T(8,128)S(1)} %cycle.1) | data formatting | bytes 1310720

commit v5 on v4

--- a/solution.py
+++ b/solution.py
@@ -152,7 +152,7 @@
     rhs, stage, inv_stage, lifts, coefs, cblocks, cinv, clifts, ccoefs, lift_tab, restrict_tab, face_tab,
     left_a, left_d, lift_h, lift_l, coef_cols, coef_sq,
     v, vpre, x_h, x_l, r_loc, cross_l, left_r, full_r, coef_raw, cross_k, left_ip, coarse_m, w1, w,
-    f_send, f_recv, c_send, c_recv, far_recv, p_send, p_recv, o_send, o_recv, coarse_h, pre,
+    z, f_send, f_recv, c_send, c_recv, far_recv, p_send, p_recv, o_send, o_recv, coarse_h, pre,
     nbr, load_sem, send_sem, recv_sem, far_send_sem, far_recv_sem,
 ):
     wide = lax.axis_index("wide")
@@ -225,6 +225,9 @@
     tail = jnp.zeros((8, RHS), f32)
     for face in range(4):
         for r in range(2):
+            for other in range(4):
+                if other != face ^ 1:
+                    far_recv[r, face, pl.ds(HALO * other + NCF, 4), :] = jnp.zeros((4, RHS), f32)
             c_send[r, face, pl.ds(16, 8), :] = tail
             p_send[r, face, pl.ds(16, 8), :] = tail
             far_recv[r, face, pl.ds(4 * HALO, 32), :] = jnp.zeros((32, RHS), f32)
@@ -253,6 +256,13 @@
         jnp.clip(sum(e * cross[e, f] for e in range(1, SLOTS)), 0, SLOTS - 1) for f in range(4)
     ]
     weight = {key: value.astype(f32) for key, value in cross.items()}
+    shared = {
+        (d, f): sum(
+            jnp.where(owner[d] == e, 1, 0) * cross[e, f] for e in range(SLOTS)
+        ).astype(f32)
+        for d in range(4)
+        for f in range(4)
+    }
 
     def transfer(send, recv, round_index, sem_row, face, target):
         return pltpu.make_async_remote_copy(
@@ -293,8 +303,8 @@
 
     def far_copy(round_index, face, other, device):
         return pltpu.make_async_remote_copy(
-            src_ref=c_send.at[round_index, face],
-            dst_ref=far_recv.at[round_index, other ^ 1, pl.ds(HALO * (face ^ 1), HALO)],
+            src_ref=c_send.at[round_index, face, pl.ds(0, NCF)],
+            dst_ref=far_recv.at[round_index, other ^ 1, pl.ds(HALO * (face ^ 1), NCF)],
             send_sem=far_send_sem.at[round_index, face, other],
             recv_sem=far_recv_sem.at[round_index, other ^ 1, face ^ 1],
             device_id=device,
@@ -413,9 +423,19 @@
         high, low = halves(product(left_d[owner[f]], rights[f]))
         cross_l[f] = jnp.concatenate([high, low], axis=1)
 
+    for face in range(4):
+        f_send[1, face] = trace(vpre, owner[face], face)
     wait_all(f_send, f_recv, 0, 0)
-    combine(cross_terms(cross_l, f_recv.at[0]), vpre, v)
-    send_fine(1, 1)
+    terms = cross_terms(cross_l, f_recv.at[0])
+    for f in range(4):
+        z[f] = terms[f]
+    for face in range(4):
+        line = f_send[1, face]
+        for f in range(4):
+            line = line - shared[face, f] * trace(z, f, face)
+        f_send[1, face] = line
+    start_all(f_send, f_recv, 1, 1)
+    combine([z[f] for f in range(4)], vpre, v)
 
     local_residual()
     for name in ("cblocks", "cinv", "clifts", "ccoefs", "lift", "restrict", "face"):
@@ -476,14 +496,16 @@
         def _():
             op_copy(face, face ^ 1).start()
 
+    left_high, left_low = halves(coarse_m[...].reshape(SLOTS * NC, 256))
+    left_m = jnp.concatenate([left_high, left_low], axis=0)
+    presweep(range(2))
+
     wait_all(f_send, f_recv, 1, 1)
     combine(cross_terms(cross_k, f_recv.at[1]), w1, w)
     for e in range(SLOTS):
         w1[e] = w[e]
     send_coarse(0, 2)
 
-    left_high, left_low = halves(coarse_m[...].reshape(SLOTS * NC, 256))
-    left_m = jnp.concatenate([left_high, left_low], axis=0)
 
     def quarters(left, right):
         high, low = halves(right)
@@ -559,7 +581,7 @@
             left_r[e] = jnp.concatenate([high, low], axis=0)
 
     correction(0)
-    presweep(range(2))
+    presweep(range(2, SLOTS))
 
     def one_step(round_index, near_row, ahead_row):
         wait_all(c_send, c_recv, round_index, near_row)
@@ -578,7 +600,6 @@
     send_coarse(1, 3)
     local_ahead(5, 1)
     correction(1)
-    presweep(range(2, SLOTS))
     combine(cross_terms(cross_l, f_recv.at[1]), vpre, vpre)
     lines = [trace(full_r, owner[face], face) for face in range(4)]
     high, low = halves(jnp.concatenate(lines, axis=0))
@@ -647,6 +668,7 @@
         vm((4, NF, 256), bf16), vm((SLOTS, 2 * NF, 256), bf16), vm((SLOTS, NF, 256), f32), vm((SLOTS, 6, NFACE, RHS), f32), vm((4, NC, 256), bf16),
         vm((SLOTS, NC, 640), bf16), vm((SLOTS, NC, 256), f32),
         vm((SLOTS, NC, RHS), f32), vm((SLOTS, NC, RHS), f32),
+        vm((4, NF, RHS), f32),
         vm((3, 4, NFACE, RHS), f32), vm((3, 4, NFACE, RHS), f32),
         vm((2, 4, HALO, RHS), f32), vm((2, 4, HALO, RHS), f32),
         vm((2, 4, 128, RHS), f32),

time: 37 us -> 36.9 us (level)
  no operation moved by 1% of the time
where the time goes in v5:
time: 36.9 us; the launch traced here: 36.8 us
  Pallas kernels  35.3 us (96%)
  local copies, waits for them, and re-layouts  0.84 us (2%)
  between operations  0.66 us (2%)
    pallas_call x1, Pallas kernels, body(): pl.pallas_call(kernel, out_shape=jax.ShapeDtypeStruct((SLOTS, NF, RHS), f...  35.3 us
    unnamed x1, local copies, waits for them, and re-layouts  0.84 us

profile of v5, /device:TPU:103, one launch (start us, length us, event | category | flops | bytes accessed | tf_op | source)
XLA Modules:
  0.0 36.8 jit_solution(1966226566819066859)
XLA Ops:
  0.7 35.3 %cycle.1 = f32[4,320,128]{2,1,0:T(8,128)S(1)} custom-call(f32[4,320,128]{2,1,0:T(8,128)} %rhs_hbm.1, f32[4,320,320]{2,1,0:T(8,128)} %blocks_hbm.1, f32[4,320,320]{2,1,0:T(8,128)} %inv_hbm.1, f32[6,80,320]{2,1,0:T(8,128)} %bitcast.4, f32[6,4,80]{2,1,0:T(4,128)} %bitcast.6, f32[4,40,40]{2,1,0:T(8,128)} %cblocks_hbm.1, f32[4,40,40]{2,1,0:T(8,128)} %cinv_hbm.1, ...), custom_call_target="tpu_custom_call" | custom-call | tf_op jit(solution)/shard_map/cycle/pallas_call | solution.py:683
  35.9 0.8 %copy.17 = f32[4,320,128]{2,1,0:T(8,128)} copy(f32[4,320,128]{2,1,0:T(8,128)S(1)} %cycle.1) | data formatting | bytes 1310720
